TPU v7x, 32 devices: a whole 2x2x4 slice. The times are simulated.
32 devices in a mesh: clip: 8 (over z, x), frame: 2 (over y), head: 2 (over core).
Axes of the slice: x: 2, y: 2, z: 4, core: 2. Of those that a mesh axis runs over, the one named last changes fastest.
Arguments:
- clips_in: bfloat16 [40, 392, 768], P('clip', 'frame'), may hold values from -6 to 6
- cached_kv: bfloat16 [40, 392, 2, 768], P('clip', 'frame', None, 'head'), may hold values from -6 to 6
- old_memory: bfloat16 [40, 98, 2, 768], P('clip', 'frame', None, 'head'), may hold values from -6 to 6
- stride_group: int32 [40], P('clip'), may hold values from 0 to 2
- memory_place: int32 [40, 4], P('clip'), may hold values from 1 to 120
- norm_gain: float32 [2, 768], replicated, may hold values from 0.5 to 1.5
- norm_shift: float32 [2, 768], replicated, may hold values from -2 to 2
- qkv_weight: bfloat16 [768, 3, 768], P(('clip', 'frame'), None, 'head'), may hold values from -0.21875 to 0.21875
- qkv_shift: float32 [3, 768], P(None, 'head'), may hold values from -2 to 2
- pool_kernel: float32 [3, 27, 96], replicated, may hold values from -1.25 to 1.25
- pool_gain: float32 [3, 96], replicated, may hold values from 0.5 to 1.5
- pool_shift: float32 [3, 96], replicated, may hold values from -2 to 2
- squeeze_kernel: float32 [2, 4, 96], replicated, may hold values from -3 to 3
- time_table: float32 [233, 96], replicated, may hold values from -0.6 to 0.6
- space_tables: float32 [2, 13, 96], replicated, may hold values from -0.6 to 0.6
- proj_weight: bfloat16 [768, 768], P('head', ('clip', 'frame')), may hold values from -0.21875 to 0.21875
- out_shift: float32 [2, 768], replicated, may hold values from -2 to 2
- up_weight: bfloat16 [768, 3072], P(('clip', 'frame'), 'head'), may hold values from -0.21875 to 0.21875
- up_shift: float32 [3072], P('head'), may hold values from -2 to 2
- down_weight: bfloat16 [3072, 768], P('head', ('clip', 'frame')), may hold values from -0.109375 to 0.109375
- cotangent: bfloat16 [40, 392, 768], P('clip', 'frame'), may hold values from -6 to 6
Outputs:
- block_out: bfloat16 [40, 392, 768], P('clip', 'frame')
- grad_in: bfloat16 [40, 392, 768], P('clip', 'frame')
- grad_norm_gain: float32 [2, 768], replicated
- grad_norm_shift: float32 [2, 768], replicated
- grad_qkv_weight: float32 [768, 3, 768], P(('clip', 'frame'), None, 'head')
- grad_qkv_shift: float32 [3, 768], P(None, 'head')
- grad_pool_kernel: float32 [3, 27, 96], replicated
- grad_pool_gain: float32 [3, 96], replicated
- grad_pool_shift: float32 [3, 96], replicated
- grad_squeeze_kernel: float32 [2, 4, 96], replicated
- grad_time_table: float32 [233, 96], replicated
- grad_space_tables: float32 [2, 13, 96], replicated
- grad_proj_weight: float32 [768, 768], P('head', ('clip', 'frame'))
- grad_out_shift: float32 [2, 768], replicated
- grad_up_weight: float32 [768, 3072], P(('clip', 'frame'), 'head')
- grad_up_shift: float32 [3072], P('head')
- grad_down_weight: float32 [3072, 768], P('head', ('clip', 'frame'))
Inputs may be any that keep to these rules, and one draw needn't show every extreme that they name: `stride_group`: the stride group g of each clip: its frames lie 2 ** (g + 1) raw frames apart. `memory_place`: for each clip, distances back in raw frames of its memory frames: first the 2 old_memory frames, then the 2 squeezed frames.
All inputs are finite; a program needn't handle non-finite values.
Results may differ from a plain program's by a relative error of at most 0.015.
Values may be sent and summed in bfloat16 or wider, within the bound.
A program may use at most 512 MiB of HBM per device.

v0:
```python
from functools import partial

import jax
import jax.numpy as jnp
import numpy as np
from jax import lax
from jax.sharding import PartitionSpec as P

FRAMES = 8
MEMF = 2


PRECISE_DOT = lax.Precision.HIGHEST


def with_halo(block, sides, width):
    for axis, dim in sides:
        count = lax.axis_size(axis)
        forward = [(i, i + 1) for i in range(count - 1)]
        backward = [(target, source) for source, target in forward]
        low = lax.ppermute(
            lax.slice_in_dim(block, block.shape[dim] - width, None, axis=dim), axis, forward
        )
        high = lax.ppermute(lax.slice_in_dim(block, 0, width, axis=dim), axis, backward)
        block = jnp.concatenate([low, block, high], axis=dim)
    return block


def layer_norm(values, gain_row, shift_row):
    average = jnp.mean(values, axis=-1, keepdims=True)
    centred = values - average
    variance = jnp.mean(centred * centred, axis=-1, keepdims=True)
    return centred * lax.rsqrt(variance + 1e-06) * gain_row + shift_row


def exact_gelu(values):
    return jax.nn.gelu(values, approximate=False)


def head_total(portion):
    return lax.psum(portion.astype(jnp.bfloat16), "head").astype(jnp.float32)


def pool_piece(padded, kernel_rows, gain_rows, shift_rows):
    frame_count = padded.shape[1] - 2
    grid_side = padded.shape[2]
    spaced = jnp.pad(padded, ((0, 0), (0, 0), (1, 1), (1, 1), (0, 0), (0, 0), (0, 0)))
    summed = jnp.zeros(padded.shape[:1] + (frame_count,) + padded.shape[2:], jnp.float32)
    for shift_frame in range(3):
        for shift_height in range(3):
            for shift_width in range(3):
                window = spaced[
                    :,
                    shift_frame : shift_frame + frame_count,
                    shift_height : shift_height + grid_side,
                    shift_width : shift_width + grid_side,
                ]
                summed = (
                    summed
                    + window
                    * kernel_rows[:, shift_frame * 9 + shift_height * 3 + shift_width][:, None, :]
                )
    return layer_norm(summed, gain_rows[:, None, :], shift_rows[:, None, :])


def relative_bias(queries, time_rows, space_rows, time_hot):
    grid_side = queries.shape[2]
    table_span = space_rows.shape[1]
    time_proj = jnp.einsum("cthwnd,rd->cthwnr", queries, time_rows, precision=PRECISE_DOT)
    time_part = jnp.einsum("cthwnr,ctkr->cthwnk", time_proj, time_hot, precision=PRECISE_DOT)
    places = jnp.arange(grid_side, dtype=jnp.int32)
    offsets = places[:, None] - places[None, :] + grid_side - 1
    space_hot = (
        offsets[:, :, None] == jnp.arange(table_span, dtype=jnp.int32)[None, None, :]
    ).astype(jnp.float32)
    height_proj = jnp.einsum("cthwnd,rd->cthwnr", queries, space_rows[0], precision=PRECISE_DOT)
    height_part = jnp.einsum("cthwnr,hkr->cthwnk", height_proj, space_hot, precision=PRECISE_DOT)
    width_proj = jnp.einsum("cthwnd,rd->cthwnr", queries, space_rows[1], precision=PRECISE_DOT)
    width_part = jnp.einsum("cthwnr,wkr->cthwnk", width_proj, space_hot, precision=PRECISE_DOT)
    return (
        time_part[..., :, None, None]
        + height_part[..., None, :, None]
        + width_part[..., None, None, :]
    )


def time_indices(stride_group, memory_place, frames_dev, query_time, table_rows):
    frame_count = lax.axis_size("frame")
    group_span = FRAMES // MEMF
    newer_count = frames_dev // group_span
    older_count = MEMF // frame_count
    is_current, current_time, memory_slot = ([], [], [])
    for block in range(frame_count):
        for inner in range(frames_dev):
            is_current.append(1)
            current_time.append(block * frames_dev + inner)
            memory_slot.append(0)
        inner = 0
        is_current.append(0)
        current_time.append(0)
        memory_slot.append(MEMF + block * newer_count + inner)
        inner = 0
        is_current.append(0)
        current_time.append(0)
        memory_slot.append(block * older_count + inner)
    is_current = np.array(is_current, np.int32)
    current_time = jnp.asarray(np.array(current_time, np.int32))
    memory_slot = np.array(memory_slot, np.int32)
    stride = jnp.left_shift(jnp.int32(2), stride_group)
    offset = 8 * (FRAMES - 1)
    current_index = (
        stride[:, None, None] * (query_time[None, :, None] - current_time[None, None, :]) + offset
    )
    places = memory_place[:, memory_slot]
    memory_index = stride[:, None, None] * query_time[None, :, None] + places[:, None, :] + offset
    chosen = jnp.where(jnp.asarray(is_current)[None, None, :] == 1, current_index, memory_index)
    return (chosen[..., None] == jnp.arange(table_rows, dtype=jnp.int32)).astype(jnp.float32)


def query_grid_of(query_four, grid_side):
    clip_count, query_rows, heads_here, head_dim = query_four.shape
    return query_four.astype(jnp.float32).reshape(
        clip_count,
        query_rows // (grid_side * grid_side),
        grid_side,
        grid_side,
        heads_here,
        head_dim,
    )


def attend_forward(
    query_four, key_part, value_part, time_hot, time_table, space_tables, softmax_scale
):
    clip_count, query_rows, heads_here, head_dim = query_four.shape
    key_total = key_part.shape[1]
    grid_side = (space_tables.shape[1] + 1) // 2
    query_grid = query_grid_of(query_four, grid_side)
    position_bias = relative_bias(query_grid, time_table, space_tables, time_hot)
    scores = (
        jnp.einsum("cqnd,cknd->cqnk", query_four, key_part, preferred_element_type=jnp.float32)
        * softmax_scale
    )
    scores = scores + position_bias.reshape(clip_count, query_rows, heads_here, key_total)
    log_total = jax.nn.logsumexp(scores, axis=-1, keepdims=True)
    attention = jnp.exp(scores - log_total)
    mixture = jnp.einsum(
        "cqnk,cknd->cqnd",
        attention.astype(jnp.bfloat16),
        value_part,
        preferred_element_type=jnp.float32,
    )
    mixture = mixture + query_four.astype(jnp.float32)
    return (mixture.astype(jnp.bfloat16), log_total)


def attend_backward(
    query_four,
    key_part,
    value_part,
    time_hot,
    time_table,
    space_tables,
    softmax_scale,
    log_total,
    attended_four,
):
    clip_count, query_rows, heads_here, head_dim = query_four.shape
    key_total = key_part.shape[1]
    grid_side = (space_tables.shape[1] + 1) // 2
    query_grid = query_grid_of(query_four, grid_side)
    bias_maker = partial(relative_bias, time_hot=time_hot)
    bias_again, bias_back = jax.vjp(bias_maker, query_grid, time_table, space_tables)
    bias_shape = bias_again.shape
    scores = (
        jnp.einsum("cqnd,cknd->cqnk", query_four, key_part, preferred_element_type=jnp.float32)
        * softmax_scale
    )
    scores = scores + bias_again.reshape(clip_count, query_rows, heads_here, key_total)
    attention = jnp.exp(scores - log_total)
    values_grad = jnp.einsum(
        "cqnk,cqnd->cknd",
        attention.astype(jnp.bfloat16),
        attended_four,
        preferred_element_type=jnp.float32,
    )
    probs_grad = jnp.einsum(
        "cqnd,cknd->cqnk", attended_four, value_part, preferred_element_type=jnp.float32
    )
    scores_grad = attention * (probs_grad - jnp.sum(attention * probs_grad, axis=-1, keepdims=True))
    scores_grad = scores_grad.astype(jnp.bfloat16)
    keys_grad = (
        jnp.einsum("cqnk,cqnd->cknd", scores_grad, query_four, preferred_element_type=jnp.float32)
        * softmax_scale
    )
    query_bias_grad, grad_time, grad_space = bias_back(
        scores_grad.astype(jnp.float32).reshape(bias_shape)
    )
    queries_grad = (
        jnp.einsum("cqnk,cknd->cqnd", scores_grad, key_part, preferred_element_type=jnp.float32)
        * softmax_scale
    )
    queries_grad = (
        queries_grad
        + attended_four.astype(jnp.float32)
        + query_bias_grad.reshape(clip_count, query_rows, heads_here, head_dim)
    )
    return (queries_grad, keys_grad, values_grad, grad_time, grad_space)


def local(
    clips_in,
    cached_kv,
    old_memory,
    stride_group,
    memory_place,
    norm_gain,
    norm_shift,
    qkv_weight,
    qkv_shift,
    pool_kernel,
    pool_gain,
    pool_shift,
    squeeze_kernel,
    time_table,
    space_tables,
    proj_weight,
    out_shift,
    up_weight,
    up_shift,
    down_weight,
    cotangent,
):
    clip_count, rows_clip, model_width = clips_in.shape
    head_width = qkv_weight.shape[2]
    head_dim = pool_gain.shape[1]
    head_count = head_width // head_dim
    grid_side = (space_tables.shape[1] + 1) // 2
    grid_cells = grid_side * grid_side
    frames_dev = rows_clip // grid_cells
    row_total = clip_count * rows_clip
    group_span = FRAMES // MEMF
    newer_rows = frames_dev // group_span * grid_cells
    softmax_scale = head_dim ** (-0.5)
    attn_full, proj_full = (
        lax.all_gather(qkv_weight, ("clip", "frame"), axis=0, tiled=True),
        lax.all_gather(proj_weight, ("clip", "frame"), axis=1, tiled=True),
    )
    qkv_flat = attn_full.reshape(model_width, 3 * head_width)
    inputs_wide = clips_in.reshape(row_total, model_width).astype(jnp.float32)
    normed_one, norm_one_back = jax.vjp(layer_norm, inputs_wide, norm_gain[0], norm_shift[0])
    rounded_one = normed_one.astype(jnp.bfloat16)
    joined = jnp.dot(rounded_one, qkv_flat, preferred_element_type=jnp.float32) + qkv_shift.reshape(
        -1
    )
    joined = joined.astype(jnp.bfloat16).reshape(clip_count, rows_clip, 3 * head_width)
    rimmed = with_halo(joined, (("frame", 1),), grid_cells)
    grid_input = rimmed.astype(jnp.float32).reshape(
        clip_count, frames_dev + 2, grid_side, grid_side, 3, head_count, head_dim
    )
    pooled, pool_back = jax.vjp(pool_piece, grid_input, pool_kernel, pool_gain, pool_shift)
    pooled_low = pooled.astype(jnp.bfloat16).reshape(clip_count, rows_clip, 3, head_width)
    cached_wide = cached_kv.astype(jnp.float32).reshape(
        clip_count, frames_dev // group_span, group_span, grid_cells, 2, head_width
    )
    tiled_kernel = jnp.tile(squeeze_kernel, (1, 1, head_count))
    squeezed = jnp.einsum("cmjsxh,xjh->cmsxh", cached_wide, tiled_kernel, precision=PRECISE_DOT)
    squeezed = squeezed.astype(jnp.bfloat16).reshape(clip_count, newer_rows, 2, head_width)
    memory_rows = jnp.concatenate([squeezed, old_memory], axis=1)
    local_keys = jnp.concatenate([pooled_low[:, :, 1:3], memory_rows], axis=1)
    all_keys = lax.all_gather(local_keys, "frame", axis=1, tiled=True)
    query_four = pooled_low[:, :, 0].reshape(clip_count, rows_clip, head_count, head_dim)
    query_time = lax.axis_index("frame") * frames_dev + jnp.arange(frames_dev, dtype=jnp.int32)
    key_total = all_keys.shape[1]
    key_part = all_keys[:, :, 0].reshape(clip_count, key_total, head_count, head_dim)
    value_part = all_keys[:, :, 1].reshape(clip_count, key_total, head_count, head_dim)
    time_hot = time_indices(stride_group, memory_place, frames_dev, query_time, time_table.shape[0])
    mixed, log_total = attend_forward(
        query_four, key_part, value_part, time_hot, time_table, space_tables, softmax_scale
    )
    attended = mixed.reshape(row_total, head_width)
    branch = (
        head_total(jnp.dot(attended, proj_full, preferred_element_type=jnp.float32)) + out_shift[0]
    )
    middle = inputs_wide + branch
    normed_two, norm_two_back = jax.vjp(layer_norm, middle, norm_gain[1], norm_shift[1])
    rounded_two = normed_two.astype(jnp.bfloat16)
    up_full, down_full = (
        lax.all_gather(up_weight, ("clip", "frame"), axis=0, tiled=True),
        lax.all_gather(down_weight, ("clip", "frame"), axis=1, tiled=True),
    )
    hidden = jnp.dot(rounded_two, up_full, preferred_element_type=jnp.float32) + up_shift
    activated, gelu_back = jax.vjp(exact_gelu, hidden)
    activated_low = activated.astype(jnp.bfloat16)
    block_out = (
        middle
        + head_total(jnp.dot(activated_low, down_full, preferred_element_type=jnp.float32))
        + out_shift[1]
    )
    block_out = block_out.astype(jnp.bfloat16).reshape(clip_count, rows_clip, model_width)
    up_back, down_back = (
        lax.all_gather(up_weight, ("clip", "frame"), axis=0, tiled=True),
        lax.all_gather(down_weight, ("clip", "frame"), axis=1, tiled=True),
    )
    attn_again, proj_back = (
        lax.all_gather(qkv_weight, ("clip", "frame"), axis=0, tiled=True),
        lax.all_gather(proj_weight, ("clip", "frame"), axis=1, tiled=True),
    )
    attn_back = attn_again.reshape(model_width, 3 * head_width)
    cotan_low = cotangent.reshape(row_total, model_width)
    cotan_wide = cotan_low.astype(jnp.float32)
    grad_down = jnp.einsum(
        "rf,rd->fd", activated_low, cotan_low, preferred_element_type=jnp.float32
    )
    active_grad = jnp.einsum("rd,fd->rf", cotan_low, down_back, preferred_element_type=jnp.float32)
    hidden_grad = gelu_back(active_grad)[0].astype(jnp.bfloat16)
    grad_up_bias = jnp.sum(hidden_grad.astype(jnp.float32), axis=0)
    grad_up = jnp.einsum("rd,rf->df", rounded_two, hidden_grad, preferred_element_type=jnp.float32)
    normed_two_grad = head_total(
        jnp.einsum("rf,df->rd", hidden_grad, up_back, preferred_element_type=jnp.float32)
    )
    middle_norm_grad, gain_two_grad, shift_two_grad = norm_two_back(normed_two_grad)
    middle_grad = cotan_wide + middle_norm_grad
    branch_grad = middle_grad.astype(jnp.bfloat16)
    grad_proj = jnp.einsum("rh,rd->hd", attended, branch_grad, preferred_element_type=jnp.float32)
    attended_grad = jnp.einsum(
        "rd,hd->rh", branch_grad, proj_back, preferred_element_type=jnp.float32
    ).astype(jnp.bfloat16)
    attended_four = attended_grad.reshape(clip_count, rows_clip, head_count, head_dim)
    queries_grad, keys_grad, values_grad, grad_time, grad_space = attend_backward(
        query_four,
        key_part,
        value_part,
        time_hot,
        time_table,
        space_tables,
        softmax_scale,
        log_total,
        attended_four,
    )
    key_value_grads = jnp.stack([keys_grad, values_grad], axis=2).reshape(
        clip_count, key_total, 2, head_width
    )
    own_key_grads = lax.psum_scatter(
        key_value_grads.astype(jnp.bfloat16), "frame", scatter_dimension=1, tiled=True
    ).astype(jnp.float32)
    current_grads = own_key_grads[:, :rows_clip]
    squeezed_grad_rows = own_key_grads[:, rows_clip : rows_clip + newer_rows]
    pooled_grad_rows = jnp.concatenate(
        [queries_grad.reshape(clip_count, rows_clip, 1, head_width), current_grads], axis=2
    )
    squeezed_grads = squeezed_grad_rows.reshape(
        clip_count, frames_dev // group_span, grid_cells, 2, head_width
    )
    tiled_grad = jnp.einsum("cmjsxh,cmsxh->xjh", cached_wide, squeezed_grads, precision=PRECISE_DOT)
    grad_squeeze = jnp.sum(tiled_grad.reshape(2, group_span, head_count, head_dim), axis=2)
    pooled_grad = pooled_grad_rows.reshape(
        clip_count, frames_dev, grid_side, grid_side, 3, head_count, head_dim
    )
    grid_grad, grad_kernel, grad_pool_gain, grad_pool_bias = pool_back(pooled_grad)
    grid_grad = grid_grad.reshape(clip_count, rows_clip + 2 * grid_cells, 3 * head_width)
    rim_rows = jnp.concatenate([grid_grad[:, :grid_cells], grid_grad[:, -grid_cells:]], axis=1)
    arrived = with_halo(rim_rows.astype(jnp.bfloat16), (("frame", 1),), grid_cells).astype(
        rim_rows.dtype
    )
    own_rows = grid_grad[:, grid_cells : grid_cells + rows_clip]
    own_rows = own_rows.at[:, :grid_cells].add(arrived[:, :grid_cells])
    own_rows = own_rows.at[:, rows_clip - grid_cells :].add(arrived[:, -grid_cells:])
    joined_grad = own_rows.reshape(row_total, 3 * head_width).astype(jnp.bfloat16)
    grad_qkv_bias = jnp.sum(joined_grad.astype(jnp.float32), axis=0).reshape(3, head_width)
    grad_qkv = jnp.einsum(
        "rd,rk->dk", rounded_one, joined_grad, preferred_element_type=jnp.float32
    ).reshape(model_width, 3, head_width)
    normed_one_grad = head_total(
        jnp.einsum("rk,dk->rd", joined_grad, attn_back, preferred_element_type=jnp.float32)
    )
    input_norm_grad, gain_one_grad, shift_one_grad = norm_one_back(normed_one_grad)
    grad_in = (
        (middle_grad + input_norm_grad)
        .astype(jnp.bfloat16)
        .reshape(clip_count, rows_clip, model_width)
    )
    qkv_shard, proj_shard = (
        lax.psum_scatter(grad_qkv, ("clip", "frame"), scatter_dimension=0, tiled=True),
        lax.psum_scatter(grad_proj, ("clip", "frame"), scatter_dimension=1, tiled=True),
    )
    up_shard, down_shard = (
        lax.psum_scatter(grad_up, ("clip", "frame"), scatter_dimension=0, tiled=True),
        lax.psum_scatter(grad_down, ("clip", "frame"), scatter_dimension=1, tiled=True),
    )
    gain_sums, shift_sums, out_sums, qkv_bias_sum, up_bias_sum = lax.psum(
        (
            jnp.stack([gain_one_grad, gain_two_grad]),
            jnp.stack([shift_one_grad, shift_two_grad]),
            jnp.stack([jnp.sum(middle_grad, axis=0), jnp.sum(cotan_wide, axis=0)]),
            grad_qkv_bias,
            grad_up_bias,
        ),
        ("clip", "frame"),
    )
    kernel_sum, pool_gain_sum, pool_bias_sum, squeeze_sum, time_sum, space_sum = lax.psum(
        (grad_kernel, grad_pool_gain, grad_pool_bias, grad_squeeze, grad_time, grad_space),
        ("clip", "frame", "head"),
    )
    return (
        block_out,
        grad_in,
        gain_sums,
        shift_sums,
        qkv_shard,
        qkv_bias_sum,
        kernel_sum,
        pool_gain_sum,
        pool_bias_sum,
        squeeze_sum,
        time_sum,
        space_sum,
        proj_shard,
        out_sums,
        up_shard,
        up_bias_sum,
        down_shard,
    )


def solution(mesh):
    return jax.shard_map(
        local,
        mesh=mesh,
        in_specs=(
            P("clip", "frame", None),
            P("clip", "frame", None, "head"),
            P("clip", "frame", None, "head"),
            P("clip"),
            P("clip", None),
            P(),
            P(),
            P(("clip", "frame"), None, "head"),
            P(None, "head"),
            P(),
            P(),
            P(),
            P(),
            P(),
            P(),
            P("head", ("clip", "frame")),
            P(),
            P(("clip", "frame"), "head"),
            P("head"),
            P("head", ("clip", "frame")),
            P("clip", "frame", None),
        ),
        out_specs=(
            P("clip", "frame", None),
            P("clip", "frame", None),
            P(),
            P(),
            P(("clip", "frame"), None, "head"),
            P(None, "head"),
            P(),
            P(),
            P(),
            P(),
            P(),
            P(),
            P("head", ("clip", "frame")),
            P(),
            P(("clip", "frame"), "head"),
            P("head"),
            P("head", ("clip", "frame")),
        ),
        check_vma=False,
    )
```

profile of v0, /device:TPU:0, one launch (start us, length us, event | category | flops | bytes accessed | tf_op | source)
XLA Modules:
  0.0 2553.5 jit_solution(601609893462982391)
XLA Ops:
  37.7 34.6 %all-gather.5.cloned.1.call-done = bf16[768,3,384]{2,0,1:T(8,128)(2,1)} async-done(((bf16[48,3,384]{2,0,1:T(8,128)(2,1)}), bf16[768,3,384]{2,0,1:T(8,128)(2,1)}) %all-gather.5.cloned.1.call-update) | async-done | bytes 1769488 | tf_op jit(solution)/shard_map/all_gather | solution.py:246
  89.8 52.1 %all_gather.21 = bf16[384,768]{0,1:T(8,128)(2,1)} all-gather(bf16[384,48]{0,1:T(8,128)(2,1)S(1)} %copy-done.64), channel_id=1, replica_groups=mesh['clip'=8,'frame'=2,'head'=2] {'clip','frame'}, dimensions={1}, use_global_device_ids=true | all-gather | bytes 626688 | tf_op jit(solution)/shard_map/all_gather | solution.py:247
  155.8 61.2 %fusion.99 = (f32[5,4,7,7,3,4]{5,4,3,2,1,0:T(4,128)S(1)}, f32[5,4,7,7,3,4,96]{6,5,4,3,2,1,0:T(4,128)}) fusion(f32[3,96]{1,0:T(4,128)S(1)} %get-tuple-element.269, f32[3,96]{1,0:T(4,128)S(1)} %get-tuple-element.270, f32[3,96]{1,0:T(4,128)S(1)} %get-tuple-element.277, f32[3,96]{1,0:T(4,128)S(1)} %get-tuple-element.278, f32[3,96]{1,0:T(4,128)S(1)} %get-tuple-element.279, ...), kind=kLoop, calls=%fused_computation.303 | loop fusion | flops 60952080 | bytes 31689024 | tf_op jit(solution)/shard_map/jvp()/reduce_sum | solution.py:30
  280.0 16.6 convolution_bitcast_fusion.1
  318.4 70.9 %broadcast_add_fusion = f32[5,4,7,7,4,12,7,7]{7,6,5,3,2,1,4,0:T(8,128)} fusion(f32[5,4,7,7,4,7]{5,3,2,1,4,0:T(8,128)S(1)} %copy-done.33, f32[5,4,7,7,4,12,7]{6,5,3,2,1,4,0:T(8,128)} %broadcast_add_fusion.1), kind=kLoop, calls=%fused_computation.1 | loop fusion | flops 2304960 | bytes 10646720 | tf_op jit(solution)/shard_map/add | solution.py:81
  390.6 234.5 %add.537 = f32[5,196,4,588]{3,1,2,0:T(8,128)} reshape(f32[5,4,7,7,4,12,7,7]{7,6,5,3,2,1,4,0:T(8,128)} %broadcast_add_fusion) | data formatting | bytes 18439680 | tf_op jit(solution)/shard_map/add | solution.py:81
  699.1 63.0 %all-gather.9.cloned.1.call-done = bf16[768,1536]{1,0:T(8,128)(2,1)} async-done(((bf16[48,1536]{1,0:T(8,128)(2,1)}), bf16[768,1536]{1,0:T(8,128)(2,1)}) %all-gather.9.cloned.1.call-update) | async-done | bytes 2359312 | tf_op jit(solution)/shard_map/all_gather | solution.py:289
  769.0 56.9 %all-gather.11.cloned.1.call-done = bf16[1536,768]{0,1:T(8,128)(2,1)} async-done(((bf16[1536,48]{0,1:T(8,128)(2,1)}), bf16[1536,768]{0,1:T(8,128)(2,1)}) %all-gather.11.cloned.1.call-update) | async-done | bytes 2359312 | tf_op jit(solution)/shard_map/all_gather | solution.py:290
  825.9 20.9 convert_reduce_fusion
  906.5 273.9 %reshape.693 = f32[5,4,7,7,4,12,7,7]{7,6,5,3,2,1,4,0:T(8,128)} reshape(bf16[5,196,4,588]{3,1,2,0:T(8,128)(2,1)} %fusion.2) | data formatting | bytes 13829760 | tf_op jit(solution)/shard_map/reshape | solution.py:197
  1215.9 343.0 %fusion.94 = (f32[5,4,7,7,4,7]{5,3,2,1,4,0:T(8,128)}, f32[5,4,7,7,4,12]{5,3,2,1,4,0:T(8,128)S(1)}, f32[5,4,7,7,4,7]{5,3,2,1,4,0:T(8,128)}) fusion(f32[5,4,7,7,4,12,7,7]{7,6,5,3,2,1,4,0:T(8,128)} %reshape.693), kind=kLoop, calls=%fused_computation.299 | loop fusion | flops 6812960 | bytes 9627520 | tf_op jit(solution)/shard_map/transpose(jvp())/reduce_sum | solution.py:81
  1625.6 20.5 fusion.97
  1648.3 20.9 multiply_reduce_fusion.26
  1669.4 38.8 %broadcast_multiply_fusion = (f32[5,4,7,7,3,4,96]{6,5,4,3,2,1,0:T(4,128)}, f32[5,4,7,7,3,4,96]{6,5,4,3,2,1,0:T(4,128)}, f32[5,4,7,7,3,4,96]{6,5,4,3,2,1,0:T(4,12...) fusion(f32[5,4,7,7,3,4,96]{6,5,4,3,2,1,0:T(4,128)} %get-tuple-e, ...), kind=kLoop, calls=%fused_computation.130 | loop fusion | flops 20321280 | bytes 85821696 | tf_op jit(solution)/shard_map/transpose(jvp())/mul | solution.py:60
  1708.4 18.1 broadcast_multiply_fusion.1
  1726.5 37.7 %pad_add_fusion = f32[5,6,9,9,3,4,96]{6,5,4,3,2,1,0:T(4,128)S(1)} fusion(f32[5,4,7,7,3,4,96]{6,5,4,3,2,1,0:T(4,128)} %get-tuple-element.206, f32[5,4,7,7,3,4,96]{6,5,4,3,2,1,0:T(4,128)} %get-tuple-element.207, f32[5,4,7,7,3,4,96]{6,5,4,3,2,1,0:T(4,128)} %get-tuple-element.208, f32[5,4,7,7,3,4,96]{6,5,4,3,2,1,0:T(4,128)} %get-tuple-element.209, ...), kind=kLoop, calls=%fused_computation.27 | loop fusion | flops 55987200 | bytes 106030080 | tf_op jit(solution)/shard_map/transpose(jvp())/add_any | solution.py:52
  1764.2 15.9 pad_add_fusion.1
  1888.8 42.4 %multiply_reduce_fusion.27 = (f32[3,96]{1,0:T(4,128)S(1)}, f32[3,96]{1,0:T(4,128)S(1)}, f32[3,96]{1,0:T(4,128)S(1)}, f32[3,96]{1,0:T(4,128)S(1)}, f32[3,96]{1,0:...) fusion(f32[5,4,7,7,3,4,96]{6,5,4,3,2,1,0:T(4,128)} %get-tuple-e, ...), kind=kLoop, calls=%fused_computation.90 | loop fusion | flops 40637376 | bytes 27115776 | tf_op jit(solution)/shard_map/transpose(jvp())/reduce_sum | solution.py:60
  1931.3 43.9 %all-reduce.58 = (f32[3,27,96]{2,0,1:T(4,128)S(1)}, f32[3,96]{1,0:T(4,128)}, f32[3,96]{1,0:T(4,128)}, f32[2,4,96]{2,1,0:T(4,128)}, f32[2,13,96]{2,1,0:T(8,128)S(1)}) all-reduce(f32[3,27,96]{2,0,1:T(4,128)S(1)} %pad_add_fusion.7, f32[3,96]{1,0:T(4,128)S(1)} %copy-done.139, ...), channel_id=1, replica_groups=mesh['clip'=8,'frame'=2,'head'=2] {'clip','frame','head'}, use_global_device_ids=true, to_apply=%region_59.60 | all-reduce | flops 11616 | bytes 92928 | tf_op jit(solution)/shard_map/psum | solution.py:401
  1994.6 76.8 %all-reduce.59 = (f32[2,768]{1,0:T(2,128)}, f32[2,768]{1,0:T(2,128)}, f32[3,384]{1,0:T(4,128)}, f32[2,768]{1,0:T(2,128)}, f32[1536]{0:T(1024)}) all-reduce(f32[2,768]{1,0:T(2,128)S(1)} %pad_maximum_fusion.6, f32[2,768]{1,0:T(2,128)S(1)} %pad_maximum_fusion.7, ...), channel_id=1, replica_groups=mesh['clip'=8,'frame'=2,'head'=2] {'clip','frame'}, use_global_device_ids=true, to_apply=%region_25.26 | all-reduce | flops 7296 | bytes 58368 | tf_op jit(solution)/shard_map/psum | solution.py:391
  2071.4 49.6 %reduce-scatter.7.cloned.1.call-done = f32[384,48]{0,1:T(8,128)} async-done(((f32[384,768]{0,1:T(8,128)}), f32[384,48]{0,1:T(8,128)}) %reduce-scatter.7.cloned.1.call-update) | async-done | bytes 73744 | tf_op jit(solution)/shard_map/reduce_scatter | solution.py:385
  2121.0 142.8 %reduce-scatter.9.cloned.1.call-done = f32[48,1536]{1,0:T(8,128)} async-done(((f32[768,1536]{1,0:T(8,128)}), f32[48,1536]{1,0:T(8,128)}) %reduce-scatter.9.cloned.1.call-update) | async-done | bytes 294928 | tf_op jit(solution)/shard_map/reduce_scatter | solution.py:388
  2263.9 141.9 %reduce-scatter.11.cloned.1.call-done = f32[1536,48]{0,1:T(8,128)} async-done(((f32[1536,768]{0,1:T(8,128)}), f32[1536,48]{0,1:T(8,128)}) %reduce-scatter.11.cloned.1.call-update) | async-done | bytes 294928 | tf_op jit(solution)/shard_map/reduce_scatter | solution.py:389
  2405.7 139.3 %reduce-scatter.5.cloned.1.call-done = f32[48,3,384]{2,0,1:T(8,128)} async-done(((f32[768,3,384]{2,0,1:T(8,128)}), f32[48,3,384]{2,0,1:T(8,128)}) %reduce-scatter.5.cloned.1.call-update) | async-done | bytes 221200 | tf_op jit(solution)/shard_map/reduce_scatter | solution.py:384
  (536 shorter events, 520.1 us)
Async XLA Ops:
  7.2 294.7 %copy-start = (f32[233,96]{0,1:T(8,128)S(1)}, f32[233,96]{0,1:T(8,128)}, u32[]{:S(2)}) copy-start(f32[233,96]{0,1:T(8,128)} %param.42) | copy-start | bytes 268420
  7.2 65.1 %all-gather.5.cloned.1.call-start = ((), (), s32[]{:S(2)}) async-start(), calls=%async_computation.4 | async-start | bytes 1880064 | tf_op jit(solution)/shard_map/all_gather | solution.py:246
  8.0 617.2 %all-gather.7.cloned.1.call-start = ((), (), s32[]{:S(2)}) async-start(), calls=%async_computation.5 | async-start | bytes 6773760 | tf_op jit(solution)/shard_map/all_gather | solution.py:271
  37.7 266.5 %copy-start.56 = (s32[5,4,12]{2,1,0:T(4,128)}, s32[5,4,12]{2,1,0:T(4,128)S(1)}, u32[]{:S(2)}) copy-start(s32[5,4,12]{2,1,0:T(4,128)S(1)} %add_select_fusion) | copy-start | bytes 2884
  83.8 58.1 %collective-permute-start.1 = (bf16[5,49,1152]{2,1,0:T(8,128)(2,1)S(1)}, bf16[5,49,1152]{2,1,0:T(8,128)(2,1)S(1)}, u32[]{:S(2)}, u32[]{:S(2)}) collective-permute-start(bf16[5,49,1152]{2,1,0:T(8,128)(2,1)S(1)} %get-tuple-element.231), channel_id=1, source_target_pairs={{2,0},{3,1},{6,4},{7,5},{10,8},{11,9},{14,12},{15,13},{18,16},{19,... | collective-permute-start | bytes 1693448 | tf_op jit(solution)/shard_map/ppermute | solution.py:24
  85.1 56.8 %collective-permute-start = (bf16[5,49,1152]{2,1,0:T(8,128)(2,1)S(1)}, bf16[5,49,1152]{2,1,0:T(8,128)(2,1)S(1)}, u32[]{:S(2)}, u32[]{:S(2)}) collective-permute-start(bf16[5,49,1152]{2,1,0:T(8,128)(2,1)S(1)} %get-tuple-element.230), channel_id=1, source_target_pairs={{0,2},{1,3},{4,6},{5,7},{8,10},{9,11},{12,14},{13,15},{16,18},{17,... | collective-permute-start | bytes 1693448 | tf_op jit(solution)/shard_map/ppermute | solution.py:21
  89.7 190.2 %copy-start.54 = (s32[7,7]{1,0:T(8,128)}, s32[7,7]{1,0:T(8,128)S(1)}, u32[]{:S(2)}) copy-start(s32[7,7]{1,0:T(8,128)S(1)} %subtract_add_fusion) | copy-start | bytes 592
  89.8 188.7 %copy-start.60 = (f32[1,13,96]{2,0,1:T(1,128)}, f32[1,13,96]{2,0,1:T(1,128)S(1)}, u32[]{:S(2)}) copy-start(f32[1,13,96]{2,0,1:T(1,128)S(1)} %get-tuple-element.259) | copy-start | bytes 14980
  255.1 440.7 %all-reduce.67.cloned.1.call-start = ((), (), s32[]{:S(2)}) async-start(), calls=%async_computation.6 | async-start | bytes 3022848 | tf_op jit(solution)/shard_map/psum | solution.py:41
  390.6 273.9 %copy-start.24 = (bf16[5,196,1,384]{1,3,0,2:T(8,128)(2,1)}, bf16[5,196,1,384]{1,3,0,2:T(8,128)(2,1)S(1)}, u32[]{:S(2)}) copy-start(bf16[5,196,1,384]{1,3,0,2:T(8,128)(2,1)S(1)} %copy.177) | copy-start | bytes 2257924
  679.4 82.6 %all-gather.9.cloned.1.call-start = ((), (), s32[]{:S(2)}) async-start(), calls=%async_computation.7 | async-start | bytes 2506752 | tf_op jit(solution)/shard_map/all_gather | solution.py:289
  680.0 145.9 %all-gather.11.cloned.1.call-start = ((), (), s32[]{:S(2)}) async-start(), calls=%async_computation.8 | async-start | bytes 2506752 | tf_op jit(solution)/shard_map/all_gather | solution.py:290
  680.6 190.9 %all-reduce.69.cloned.1.call-start = ((), (), s32[]{:S(2)}) async-start(), calls=%async_computation.9 | async-start | bytes 3022848 | tf_op jit(solution)/shard_map/psum | solution.py:41
  852.3 744.4 %all-reduce.73.cloned.1.call-start = ((), (), s32[]{:S(2)}) async-start(), calls=%async_computation.15 | async-start | bytes 9031680
  906.5 273.9 %copy-start.25 = (bf16[5,196,1,384]{1,3,0,2:T(8,128)(2,1)S(1)}, bf16[5,196,1,384]{1,3,0,2:T(8,128)(2,1)}, u32[]{:S(2)}) copy-start(bf16[5,196,1,384]{1,3,0,2:T(8,128)(2,1)} %copy-done.24) | copy-start | bytes 2257924
  1215.9 343.0 %copy-start.55 = (s32[7,7]{1,0:T(8,128)S(1)}, s32[7,7]{1,0:T(8,128)}, u32[]{:S(2)}) copy-start(s32[7,7]{1,0:T(8,128)} %copy-done.54) | copy-start | bytes 592
  1215.9 760.6 %all-reduce.75.cloned.1.call-start = ((), (), s32[]{:S(2)}) async-start(), calls=%async_computation.16 | async-start | bytes 6045696 | tf_op jit(solution)/shard_map/psum | solution.py:41
  1793.8 18.5 collective-permute-start.3
  1795.1 18.7 collective-permute-start.2
  1836.2 235.3 %all-reduce.71.cloned.1.call-start = ((), (), s32[]{:S(2)}) async-start(), calls=%async_computation.11 | async-start | bytes 196608 | tf_op jit(solution)/shard_map/psum | solution.py:401
  1842.7 278.3 %reduce-scatter.7.cloned.1.call-start = ((), (), s32[]{:S(2)}) async-start(), calls=%async_computation.12 | async-start | bytes 1253376 | tf_op jit(solution)/shard_map/reduce_scatter | solution.py:385
  1847.3 416.5 %reduce-scatter.9.cloned.1.call-start = ((), (), s32[]{:S(2)}) async-start(), calls=%async_computation.13 | async-start | bytes 5013504 | tf_op jit(solution)/shard_map/reduce_scatter | solution.py:388
  1854.2 551.5 %reduce-scatter.11.cloned.1.call-start = ((), (), s32[]{:S(2)}) async-start(), calls=%async_computation.14 | async-start | bytes 5013504 | tf_op jit(solution)/shard_map/reduce_scatter | solution.py:389
  1861.6 683.4 %reduce-scatter.5.cloned.1.call-start = ((), (), s32[]{:S(2)}) async-start(), calls=%async_computation.10 | async-start | bytes 3760128 | tf_op jit(solution)/shard_map/reduce_scatter | solution.py:384
  (154 other events, 6416.3 us)
Sparse Core Ops, SparseCore 0:
  10.7 61.5 all-gather.4
  255.2 56.2 all-gather.6
  679.6 16.1 all-reduce.66
  698.4 63.5 all-gather.8
  764.7 61.1 all-gather.10
  852.4 19.1 all-reduce.68
  1216.0 116.0 all-reduce.72
  1836.2 25.3 all-reduce.74
  1868.7 121.7 all-reduce.70
  1996.3 124.6 reduce-scatter.6
  2127.6 136.2 reduce-scatter.8
  2269.5 136.2 reduce-scatter.10
  2412.2 132.7 reduce-scatter.4
where the time goes:
time: 2560 us; the launch traced here: 2550 us
  other arithmetic  799 us (31%)
  local copies, waits for them, and re-layouts  707 us (28%)
  waiting for transfers between devices  658 us (26%)
  matrix products  185 us (7%)
  blocking collectives  173 us (7%)
    reduce_sum x1, other arithmetic, relative_bias(): time_part[..., :, None, None] + height_part[..., None, :, None]  343 us
    reshape x1, local copies, waits for them, and re-layouts, attend_backward(): scores_grad.astype(jnp.float32).reshape(bias_shape)  274 us
    add x1, local copies, waits for them, and re-layouts, relative_bias(): time_part[..., :, None, None] + height_part[..., None, :, None]  235 us
    reduce_scatter x1, waiting for transfers between devices, local(): lax.psum_scatter(grad_up, ('clip', 'frame'), scatter_dimension=0, tiled=T...  143 us
    reduce_scatter x1, waiting for transfers between devices, local(): lax.psum_scatter(grad_down, ('clip', 'frame'), scatter_dimension=1, tiled...  142 us
    reduce_scatter x1, waiting for transfers between devices, local(): lax.psum_scatter(grad_qkv, ('clip', 'frame'), scatter_dimension=0, tiled=...  139 us
    add x2, other arithmetic, relative_bias(): time_part[..., :, None, None] + height_part[..., None, :, None]  82.1 us
    psum x1, blocking collectives, local(): lax.psum((jnp.stack([gain_one_grad, gain_two_grad]), jnp.stack([shift_one...  76.8 us
  transfers between devices with their start and end apart: 17, of which 11 were waited for; matrix products, arithmetic and copies ran while one was open for 36% of the time, Pallas kernels for 0%

commit v1 on v0

v1 whole, which is shorter than its diff:
```python
from functools import partial

import jax
import jax.numpy as jnp
import numpy as np
from jax import lax
from jax.experimental import pallas as pl
from jax.experimental.pallas import tpu as pltpu
from jax.sharding import PartitionSpec as P

FRAMES = 8
MEMF = 2
SIDE = 7
CELLS = SIDE * SIDE
LANES = 128
HALF = 208
QROWS = 2 * HALF
GRID_ROWS = FRAMES * SIDE * 8
MEM_AT = QROWS
MEM_PAD = 112
KROWS = 640
BIAS_COLS = 256
SPACE_AT = 128
PAD_LANE = 127
BF = jnp.bfloat16
F32 = jnp.float32
VMEM_LIMIT = 60 * 1024 * 1024


def dot_f32(a, b, dims):
    return lax.dot_general(a, b, (dims, ((), ())), preferred_element_type=F32)


def frame_order(first, own):
    rest = [t for t in range(FRAMES) if not first * own <= t < (first + 1) * own]
    return list(range(first * own, (first + 1) * own)) + rest


def placement(frame_count):
    own = FRAMES // frame_count
    into = np.zeros((frame_count, GRID_ROWS, QROWS), np.float32)
    for first in range(frame_count):
        for slot, frame in enumerate(frame_order(first, own)):
            base = (slot // own) * HALF + (slot % own) * CELLS
            for high in range(SIDE):
                for wide in range(SIDE):
                    row = (frame * SIDE + high) * 8 + wide
                    into[first, row, base + high * SIDE + wide] = 1.0
    return into, np.ascontiguousarray(into.transpose(0, 2, 1))


def bias_constants(frame_count):
    own = FRAMES // frame_count
    frames_all = FRAMES + 2 * MEMF
    keys = np.zeros((BIAS_COLS, KROWS), np.float32)
    valid = np.zeros((KROWS,), bool)

    def mark(col, slot, high, wide):
        valid[col] = True
        for query in range(FRAMES):
            keys[query * frames_all + slot, col] = 1.0
        for place in range(SIDE):
            keys[SPACE_AT + place * SIDE + high, col] = 1.0
            keys[SPACE_AT + CELLS + place * SIDE + wide, col] = 1.0

    mask = np.zeros((QROWS, BIAS_COLS), np.float32)
    for slot in range(FRAMES):
        base = (slot // own) * HALF + (slot % own) * CELLS
        for high in range(SIDE):
            for wide in range(SIDE):
                row = base + high * SIDE + wide
                mark(row, slot, high, wide)
                mask[row, slot * frames_all : (slot + 1) * frames_all] = 1.0
                mask[row, SPACE_AT + high * SIDE : SPACE_AT + (high + 1) * SIDE] = 1.0
                low = SPACE_AT + CELLS + wide * SIDE
                mask[row, low : low + SIDE] = 1.0
    for group in range(2):
        for inner in range(MEMF):
            slot = FRAMES + group * MEMF + inner
            for high in range(SIDE):
                for wide in range(SIDE):
                    col = MEM_AT + group * MEM_PAD + inner * CELLS + high * SIDE + wide
                    mark(col, slot, high, wide)
    keys[PAD_LANE, ~valid] = -1e9
    pad_row = np.zeros((1, BIAS_COLS), np.float32)
    pad_row[0, PAD_LANE] = 1.0
    return keys, mask, pad_row


def spread_heads(source, target, rows_at, units, unit, first=0):
    count = source.shape[1]
    for index in range(units):
        at = (first + index) * unit
        target[rows_at : rows_at + count, index * LANES : index * LANES + unit] = source[
            0, :, at : at + unit
        ]


def load_shifted(field, shifted):
    grid = field.reshape(FRAMES, SIDE, 8, field.shape[-1])
    flat = field.reshape(FRAMES * SIDE, 8, field.shape[-1])
    shifted[1, 1 : FRAMES + 1, 1 : SIDE + 1] = grid
    shifted[0, 1 : FRAMES + 1, 1 : SIDE + 1] = pltpu.roll(flat, 1, 1).reshape(grid.shape)
    shifted[2, 1 : FRAMES + 1, 1 : SIDE + 1] = pltpu.roll(flat, 7, 1).reshape(grid.shape)


def convolve(shifted, taps, target, flip):
    tiles = target.shape[-1] // LANES

    def step(index, carry):
        frame = index // tiles
        lanes = pl.ds(pl.multiple_of((index % tiles) * LANES, LANES), LANES)
        total = jnp.zeros((SIDE, 8, LANES), F32)
        for i in range(3):
            for k in range(3):
                rows = shifted[k, frame + i, :, :, lanes]
                for j in range(3):
                    if flip:
                        tap = (2 - i) * 9 + (2 - j) * 3 + (2 - k)
                    else:
                        tap = i * 9 + j * 3 + k
                    total = total + rows[j : j + SIDE] * taps[tap, :, lanes][None]
        target[frame, :, :, lanes] = total
        return carry

    lax.fori_loop(0, FRAMES * tiles, step, 0)


def tap_grads(shifted, grads, target):
    tiles = target.shape[-1] // LANES
    for i in range(3):

        def step(index, carry, i=i):
            lanes = pl.ds(pl.multiple_of(index * LANES, LANES), LANES)

            def inner(frame, sums):
                centre = grads[frame + 1, :, :, lanes]
                new = []
                for j in range(3):
                    for k in range(3):
                        rows = shifted[k, frame + i, j : j + SIDE, :, lanes]
                        new.append(sums[j * 3 + k] + jnp.sum(rows * centre[1 : SIDE + 1], axis=0))
                return tuple(new)

            start = tuple(jnp.zeros((8, LANES), F32) for _ in range(9))
            sums = lax.fori_loop(0, FRAMES, inner, start)
            for tap in range(9):
                target[i * 9 + tap, :, lanes] += sums[tap]
            return carry

        lax.fori_loop(0, tiles, step, 0)


def head_stats(values, unit):
    average = jnp.sum(values, axis=-1, keepdims=True) * (1.0 / unit)
    lane = lax.broadcasted_iota(jnp.int32, values.shape, 1)
    centred = jnp.where(lane < unit, values - average, 0.0)
    variance = jnp.sum(centred * centred, axis=-1, keepdims=True) * (1.0 / unit)
    return centred, lax.rsqrt(variance + 1e-06)


def forward_kernel(
    which, own_ref, peer_ref, mem_own_ref, mem_peer_ref, into_ref, outof_ref, taps_ref, gain_ref,
    shift_ref, bias_ref, keyhot_ref, mask_ref, pad_ref,
    out_own, out_peer, q_out, k_out, v_out, p_out, c_out,
    packed, shifted, taps, *, heads, unit, scale,
):
    units = 3 * heads
    own_rows = own_ref.shape[1]

    @pl.when(pl.program_id(0) == 0)
    def _():
        packed[...] = jnp.zeros_like(packed)
        shifted[...] = jnp.zeros_like(shifted)
        for tap in range(27):
            taps[tap] = jnp.broadcast_to(taps_ref[tap : tap + 1], taps.shape[1:])

    spread_heads(own_ref, packed, 0, units, unit)
    spread_heads(peer_ref, packed, HALF, units, unit)
    field = dot_f32(into_ref[0], packed[...], ((1,), (0,)))
    load_shifted(field, shifted)
    conv = c_out.at[0]
    convolve(shifted, taps, conv, False)
    k_out[0, MEM_AT:, :] = jnp.zeros((KROWS - MEM_AT, heads * LANES), BF)
    v_out[0, MEM_AT:, :] = jnp.zeros((KROWS - MEM_AT, heads * LANES), BF)
    spread_heads(mem_own_ref, k_out.at[0], MEM_AT, heads, unit, 0 * heads)
    spread_heads(mem_own_ref, v_out.at[0], MEM_AT, heads, unit, 1 * heads)
    spread_heads(mem_peer_ref, k_out.at[0], MEM_AT + MEM_PAD, heads, unit, 0 * heads)
    spread_heads(mem_peer_ref, v_out.at[0], MEM_AT + MEM_PAD, heads, unit, 1 * heads)
    for index in range(units):
        lanes = slice(index * LANES, (index + 1) * LANES)
        block = conv[:, :, :, lanes].reshape(GRID_ROWS, LANES)
        centred, rate = head_stats(block, unit)
        normal = centred * rate * gain_ref[:, lanes] + shift_ref[:, lanes]
        rows = dot_f32(outof_ref[0], normal.astype(BF), ((1,), (0,))).astype(BF)
        target = (q_out, k_out, v_out)[index // heads]
        local = slice((index % heads) * LANES, (index % heads + 1) * LANES)
        target[0, 0:QROWS, local] = rows

    bias = bias_ref[0]
    bias_high = bias.astype(BF)
    bias_low = (bias - bias_high.astype(F32)).astype(BF)
    for head in range(heads):
        lanes = slice(head * LANES, (head + 1) * LANES)
        keys = k_out[0, :, lanes]
        values = v_out[0, :, lanes]
        for half in range(2):
            rows = slice(half * HALF, (half + 1) * HALF)
            query = q_out[0, rows, lanes]
            table = dot_f32(query, bias_high, ((1,), (1,))) + dot_f32(query, bias_low, ((1,), (1,)))
            table = table * mask_ref[rows, :] + pad_ref[...]
            table_high = table.astype(BF)
            table_low = (table - table_high.astype(F32)).astype(BF)
            scores = dot_f32(query, keys, ((1,), (1,)))
            scores = scores + dot_f32(table_high, keyhot_ref[...], ((1,), (0,)))
            scores = scores + dot_f32(table_low, keyhot_ref[...], ((1,), (0,)))
            top = jnp.max(scores, axis=-1, keepdims=True)
            weights = jnp.exp((scores - top) * scale)
            total = jnp.sum(weights, axis=-1, keepdims=True)
            probs = (weights * (1.0 / total)).astype(BF)
            p_out[0, head, rows, :] = probs
            mixed = dot_f32(probs, values, ((1,), (0,))) + query.astype(F32)
            target = (out_own, out_peer)[half]
            target[0, :, head * unit : (head + 1) * unit] = mixed[:own_rows, :unit].astype(BF)


def backward_kernel(
    which, own_ref, peer_ref, grad_own_ref, grad_peer_ref, into_ref, outof_ref, taps_ref, gain_ref,
    bias_ref, keyhot_ref, mask_ref, q_ref, k_ref, v_ref, p_ref, c_ref,
    out_own, out_peer, mem_own, mem_peer, taps_out, gain_out, shift_out, bias_out,
    packed, shifted, taps, grads, spread, pooled, *, heads, unit, scale,
):
    units = 3 * heads
    own_rows = own_ref.shape[1]

    @pl.when(pl.program_id(0) == 0)
    def _():
        packed[...] = jnp.zeros_like(packed)
        shifted[...] = jnp.zeros_like(shifted)
        grads[...] = jnp.zeros_like(grads)
        spread[...] = jnp.zeros_like(spread)
        taps_out[...] = jnp.zeros_like(taps_out)
        gain_out[...] = jnp.zeros_like(gain_out)
        shift_out[...] = jnp.zeros_like(shift_out)
        for tap in range(27):
            taps[tap] = jnp.broadcast_to(taps_ref[tap : tap + 1], taps.shape[1:])

    spread_heads(own_ref, packed, 0, units, unit)
    spread_heads(peer_ref, packed, HALF, units, unit)
    load_shifted(dot_f32(into_ref[0], packed[...], ((1,), (0,))), shifted)
    spread_heads(grad_own_ref, spread, 0, heads, unit)
    spread_heads(grad_peer_ref, spread, HALF, heads, unit)
    bias_low = bias_ref[0].astype(BF)
    bias_sum = jnp.zeros((BIAS_COLS, LANES), F32)
    for head in range(heads):
        lanes = slice(head * LANES, (head + 1) * LANES)
        keys = k_ref[0, :, lanes]
        values = v_ref[0, :, lanes]
        keys_grad = jnp.zeros((KROWS, LANES), F32)
        values_grad = jnp.zeros((KROWS, LANES), F32)
        for half in range(2):
            rows = slice(half * HALF, (half + 1) * HALF)
            query = q_ref[0, rows, lanes]
            out_grad = spread[rows, lanes]
            probs = p_ref[0, head, rows, :]
            wide = probs.astype(F32)
            probs_grad = dot_f32(out_grad, values, ((1,), (1,)))
            weighted = wide * probs_grad
            shared = jnp.sum(weighted, axis=-1, keepdims=True)
            score_grad = (weighted - wide * shared).astype(BF)
            values_grad = values_grad + dot_f32(probs, out_grad, ((0,), (0,)))
            keys_grad = keys_grad + dot_f32(score_grad, query, ((0,), (0,)))
            table_grad = dot_f32(score_grad, keyhot_ref[...], ((1,), (1,))) * mask_ref[rows, :]
            table_low = table_grad.astype(BF)
            query_grad = dot_f32(score_grad, keys, ((1,), (0,)))
            query_grad = query_grad + dot_f32(table_low, bias_low, ((1,), (0,)))
            query_grad = query_grad * scale + out_grad.astype(F32)
            pooled[rows, lanes] = query_grad.astype(BF)
            bias_sum = bias_sum + dot_f32(table_low, query, ((0,), (0,)))
        keys_grad = (keys_grad * scale).astype(BF)
        values_grad = values_grad.astype(BF)
        for member, part in enumerate((keys_grad, values_grad)):
            at = ((member + 1) * heads + head) * LANES
            pooled[:, at : at + LANES] = part[:QROWS]
            at = (member * heads + head) * LANES
            mem_own[0, :, at : at + LANES] = part[MEM_AT : MEM_AT + MEM_PAD]
            mem_peer[0, :, at : at + LANES] = part[MEM_AT + MEM_PAD : MEM_AT + 2 * MEM_PAD]
    bias_out[0] = bias_sum

    for index in range(units):
        lanes = slice(index * LANES, (index + 1) * LANES)
        incoming = dot_f32(into_ref[0], pooled[:, lanes], ((1,), (0,)))
        block = c_ref[0, :, :, :, lanes].reshape(GRID_ROWS, LANES)
        centred, rate = head_stats(block, unit)
        normal = centred * rate
        product = incoming * normal
        gain_out[:, lanes] += jnp.sum(product, axis=0, keepdims=True)
        shift_out[:, lanes] += jnp.sum(incoming, axis=0, keepdims=True)
        inner = incoming * gain_ref[:, lanes]
        mean_inner = jnp.sum(inner, axis=-1, keepdims=True) * (1.0 / unit)
        mean_both = jnp.sum(inner * normal, axis=-1, keepdims=True) * (1.0 / unit)
        lane = lax.broadcasted_iota(jnp.int32, block.shape, 1)
        result = rate * (inner - mean_inner - normal * mean_both)
        result = jnp.where(lane < unit, result, 0.0)
        flat = result.reshape(FRAMES * SIDE, 8, LANES)
        shape = (FRAMES, SIDE, 8, LANES)
        grads[1, 1 : FRAMES + 1, 1 : SIDE + 1, :, lanes] = flat.reshape(shape)
        grads[0, 1 : FRAMES + 1, 1 : SIDE + 1, :, lanes] = pltpu.roll(flat, 1, 1).reshape(shape)
        grads[2, 1 : FRAMES + 1, 1 : SIDE + 1, :, lanes] = pltpu.roll(flat, 7, 1).reshape(shape)

    tap_grads(shifted, grads.at[1], taps_out)
    conv = shifted.at[1, 1 : FRAMES + 1, 1 : SIDE + 1]
    convolve(grads, taps, conv, True)
    for index in range(units):
        lanes = slice(index * LANES, (index + 1) * LANES)
        block = shifted[1, 1 : FRAMES + 1, 1 : SIDE + 1, :, lanes].reshape(GRID_ROWS, LANES)
        rows = dot_f32(outof_ref[0], block.astype(BF), ((1,), (0,))).astype(BF)
        local = slice(index * unit, (index + 1) * unit)
        out_own[0, :, local] = rows[:own_rows, :unit]
        out_peer[0, :, local] = rows[HALF : HALF + own_rows, :unit]


def whole_spec(shape):
    return pl.BlockSpec(shape, lambda clip, which: (0,) * len(shape))


def clip_spec(shape):
    return pl.BlockSpec((1,) + shape, lambda clip, which: (clip,) + (0,) * len(shape))


def frame_spec(shape):
    return pl.BlockSpec((1,) + shape, lambda clip, which: (which[0],) + (0,) * len(shape))


def attention_forward(
    which, own, peer, mem_own, mem_peer, consts, taps, gains, shifts, bias, scale, unit
):
    clips, rows, width = own.shape
    heads = width // (3 * unit)
    into, outof, keyhot, mask, pad_row = consts
    wide = 3 * heads * LANES
    mem_shape = mem_own.shape[1:]
    out = jax.ShapeDtypeStruct
    return pl.pallas_call(
        partial(forward_kernel, heads=heads, unit=unit, scale=scale),
        grid_spec=pltpu.PrefetchScalarGridSpec(
            num_scalar_prefetch=1,
            grid=(clips,),
            in_specs=[
                clip_spec((rows, width)),
                clip_spec((rows, width)),
                clip_spec(mem_shape),
                clip_spec(mem_shape),
                frame_spec((GRID_ROWS, QROWS)),
                frame_spec((QROWS, GRID_ROWS)),
                whole_spec((27, wide)),
                whole_spec((1, wide)),
                whole_spec((1, wide)),
                clip_spec((BIAS_COLS, LANES)),
                whole_spec((BIAS_COLS, KROWS)),
                whole_spec((QROWS, BIAS_COLS)),
                whole_spec((1, BIAS_COLS)),
            ],
            out_specs=[
                clip_spec((rows, heads * unit)),
                clip_spec((rows, heads * unit)),
                clip_spec((QROWS, heads * LANES)),
                clip_spec((KROWS, heads * LANES)),
                clip_spec((KROWS, heads * LANES)),
                clip_spec((heads, QROWS, KROWS)),
                clip_spec((FRAMES, SIDE, 8, wide)),
            ],
            scratch_shapes=[
                pltpu.VMEM((QROWS, wide), BF),
                pltpu.VMEM((3, FRAMES + 2, SIDE + 2, 8, wide), F32),
                pltpu.VMEM((27, 8, wide), F32),
            ],
        ),
        out_shape=[
            out((clips, rows, heads * unit), BF),
            out((clips, rows, heads * unit), BF),
            out((clips, QROWS, heads * LANES), BF),
            out((clips, KROWS, heads * LANES), BF),
            out((clips, KROWS, heads * LANES), BF),
            out((clips, heads, QROWS, KROWS), BF),
            out((clips, FRAMES, SIDE, 8, wide), F32),
        ],
        compiler_params=pltpu.CompilerParams(vmem_limit_bytes=VMEM_LIMIT),
        name="pooled_attention_forward",
    )(which, own, peer, mem_own, mem_peer, into, outof, taps, gains, shifts, bias, keyhot, mask, pad_row)


def attention_backward(
    which, own, peer, grad_own, grad_peer, consts, taps, gains, bias, saved, scale, unit
):
    clips, rows, width = own.shape
    heads = width // (3 * unit)
    into, outof, keyhot, mask, pad_row = consts
    wide = 3 * heads * LANES
    out = jax.ShapeDtypeStruct
    return pl.pallas_call(
        partial(backward_kernel, heads=heads, unit=unit, scale=scale),
        grid_spec=pltpu.PrefetchScalarGridSpec(
            num_scalar_prefetch=1,
            grid=(clips,),
            in_specs=[
                clip_spec((rows, width)),
                clip_spec((rows, width)),
                clip_spec((rows, heads * unit)),
                clip_spec((rows, heads * unit)),
                frame_spec((GRID_ROWS, QROWS)),
                frame_spec((QROWS, GRID_ROWS)),
                whole_spec((27, wide)),
                whole_spec((1, wide)),
                clip_spec((BIAS_COLS, LANES)),
                whole_spec((BIAS_COLS, KROWS)),
                whole_spec((QROWS, BIAS_COLS)),
                clip_spec((QROWS, heads * LANES)),
                clip_spec((KROWS, heads * LANES)),
                clip_spec((KROWS, heads * LANES)),
                clip_spec((heads, QROWS, KROWS)),
                clip_spec((FRAMES, SIDE, 8, wide)),
            ],
            out_specs=[
                clip_spec((rows, width)),
                clip_spec((rows, width)),
                clip_spec((MEM_PAD, 2 * heads * LANES)),
                clip_spec((MEM_PAD, 2 * heads * LANES)),
                whole_spec((27, 8, wide)),
                whole_spec((1, wide)),
                whole_spec((1, wide)),
                clip_spec((BIAS_COLS, LANES)),
            ],
            scratch_shapes=[
                pltpu.VMEM((QROWS, wide), BF),
                pltpu.VMEM((3, FRAMES + 2, SIDE + 2, 8, wide), F32),
                pltpu.VMEM((27, 8, wide), F32),
                pltpu.VMEM((3, FRAMES + 2, SIDE + 2, 8, wide), F32),
                pltpu.VMEM((QROWS, heads * LANES), BF),
                pltpu.VMEM((QROWS, wide), BF),
            ],
        ),
        out_shape=[
            out((clips, rows, width), BF),
            out((clips, rows, width), BF),
            out((clips, MEM_PAD, 2 * heads * LANES), BF),
            out((clips, MEM_PAD, 2 * heads * LANES), BF),
            out((27, 8, wide), F32),
            out((1, wide), F32),
            out((1, wide), F32),
            out((clips, BIAS_COLS, LANES), F32),
        ],
        compiler_params=pltpu.CompilerParams(vmem_limit_bytes=VMEM_LIMIT),
        name="pooled_attention_backward",
    )(which, own, peer, grad_own, grad_peer, into, outof, taps, gains, bias, keyhot, mask, *saved)


def layer_norm(values, gain_row, shift_row):
    average = jnp.mean(values, axis=-1, keepdims=True)
    centred = values - average
    variance = jnp.mean(centred * centred, axis=-1, keepdims=True)
    return centred * lax.rsqrt(variance + 1e-06) * gain_row + shift_row


def exact_gelu(values):
    return jax.nn.gelu(values, approximate=False)


def swap(value, axis):
    return lax.ppermute(value, axis, [(0, 1), (1, 0)])


def head_total(portion):
    low = portion.astype(BF)
    return low.astype(F32) + swap(low, "head").astype(F32)


def precise(pattern, *operands):
    return jnp.einsum(pattern, *operands, precision=lax.Precision.HIGHEST)


def split_groups(value, which, axis):
    half = value.shape[axis] // 2
    low = lax.slice_in_dim(value, 0, half, axis=axis)
    high = lax.slice_in_dim(value, half, None, axis=axis)
    first = which == 0
    return jnp.where(first, low, high), jnp.where(first, high, low)


def join_groups(own, peer, which, axis):
    first = which == 0
    return jnp.concatenate([jnp.where(first, own, peer), jnp.where(first, peer, own)], axis=axis)


def time_choices(stride_group, memory_place, which, own, table_rows):
    local = jnp.arange(own, dtype=jnp.int32)
    times = jnp.concatenate([which * own + local, (1 - which) * own + local])
    stride = jnp.left_shift(jnp.int32(2), stride_group)[:, None, None]
    offset = 8 * (FRAMES - 1)
    current = stride * (times[None, :, None] - times[None, None, :]) + offset
    first = memory_place[:, np.array([2, 0, 3, 1])]
    second = memory_place[:, np.array([3, 1, 2, 0])]
    places = jnp.where(which == 0, first, second)
    memory = stride * times[None, :, None] + places[:, None, :] + offset
    chosen = jnp.concatenate([current, memory], axis=2)
    return (chosen[..., None] == jnp.arange(table_rows, dtype=jnp.int32)).astype(F32)


def space_choices():
    places = np.arange(SIDE)
    offsets = places[:, None] - places[None, :] + SIDE - 1
    hot = offsets.reshape(-1)[:, None] == np.arange(2 * SIDE - 1)[None, :]
    return jnp.asarray(hot.astype(np.float32))


def wide_rows(rows, heads):
    count, members, unit = rows.shape
    padded = jnp.pad(rows, ((0, 0), (0, 0), (0, LANES - unit)))
    spread = jnp.broadcast_to(padded[:, :, None], (count, members, heads, LANES))
    return spread.reshape(count, members * heads * LANES)


def local(
    clips_in,
    cached_kv,
    old_memory,
    stride_group,
    memory_place,
    norm_gain,
    norm_shift,
    qkv_weight,
    qkv_shift,
    pool_kernel,
    pool_gain,
    pool_shift,
    squeeze_kernel,
    time_table,
    space_tables,
    proj_weight,
    out_shift,
    up_weight,
    up_shift,
    down_weight,
    cotangent,
):
    clip_count, rows_clip, model_width = clips_in.shape
    head_width = qkv_weight.shape[2]
    unit = pool_gain.shape[1]
    head_count = head_width // unit
    frame_count = lax.axis_size("frame")
    heads = head_count // frame_count
    own_frames = rows_clip // CELLS
    row_total = clip_count * rows_clip
    hidden_width = up_weight.shape[1]
    group_width = heads * unit
    group_span = FRAMES // MEMF
    scale = unit ** (-0.5)
    both = ("clip", "frame")
    which = lax.axis_index("frame")
    which_row = which.astype(jnp.int32).reshape(1)
    into_np, outof_np = placement(frame_count)
    keys_np, mask_np, pad_np = bias_constants(frame_count)
    consts = (
        jnp.asarray(into_np, BF),
        jnp.asarray(outof_np, BF),
        jnp.asarray(keys_np, BF),
        jnp.asarray(mask_np),
        jnp.asarray(pad_np),
    )

    attn_full = lax.all_gather(qkv_weight, both, axis=0, tiled=True)
    shards = jnp.concatenate([proj_weight.T, up_weight, down_weight.T], axis=1)
    rest_full = lax.all_gather(shards, both, axis=0, tiled=True)
    proj_full = rest_full[:, :head_width]
    up_full = rest_full[:, head_width : head_width + hidden_width]
    down_full = rest_full[:, head_width + hidden_width :]

    cached_wide = cached_kv.astype(F32).reshape(
        clip_count, group_span, CELLS, 2, head_count, unit
    )
    squeezed = precise("cjsxnd,xjd->csxnd", cached_wide, squeeze_kernel).astype(BF)
    memory_rows = jnp.concatenate(
        [squeezed.reshape(clip_count, CELLS, 2, head_width), old_memory], axis=1
    )
    mem_own, mem_send = split_groups(memory_rows, which, 3)
    mem_own = mem_own.reshape(clip_count, -1, 2 * group_width)
    mem_send = mem_send.reshape(clip_count, -1, 2 * group_width)
    mem_peer = swap(mem_send, "frame")

    time_hot = time_choices(stride_group, memory_place, which, own_frames, time_table.shape[0])
    time_rows = precise("ctkr,rd->ctkd", time_hot, time_table).reshape(clip_count, -1, unit)
    space_hot = space_choices()
    space_rows = precise("pr,xrd->xpd", space_hot, space_tables).reshape(2 * CELLS, unit)
    bias = jnp.zeros((clip_count, BIAS_COLS, LANES), F32)
    bias = bias.at[:, : time_rows.shape[1], :unit].set(time_rows)
    bias = bias.at[:, SPACE_AT : SPACE_AT + 2 * CELLS, :unit].set(space_rows[None])
    bias = bias * (1.0 / scale)
    taps = wide_rows(pool_kernel.transpose(1, 0, 2), heads)
    gains = wide_rows(pool_gain[None], heads)
    shifts = wide_rows(pool_shift[None], heads)

    inputs_wide = clips_in.reshape(row_total, model_width).astype(F32)
    normed_one, norm_one_back = jax.vjp(layer_norm, inputs_wide, norm_gain[0], norm_shift[0])
    rounded_one = normed_one.astype(BF)
    attn_own, attn_send = split_groups(attn_full, which, 2)
    shift_own, shift_send = split_groups(qkv_shift, which, 1)

    def project(weight, shift):
        flat = weight.reshape(model_width, 3 * group_width)
        result = jnp.dot(rounded_one, flat, preferred_element_type=F32) + shift.reshape(-1)
        return result.astype(BF).reshape(clip_count, rows_clip, 3 * group_width)

    joined_peer = swap(project(attn_send, shift_send), "frame")
    joined_own = project(attn_own, shift_own)
    forward = attention_forward(
        which_row, joined_own, joined_peer, mem_own, mem_peer, consts, taps, gains, shifts, bias,
        scale, unit,
    )
    attended_own, attended_send = forward[:2]
    saved = forward[2:]
    attended_peer = swap(attended_send, "frame")
    attended = join_groups(attended_own, attended_peer, which, 2).reshape(row_total, head_width)
    branch = head_total(dot_f32(attended, proj_full, ((1,), (1,)))) + out_shift[0]
    middle = inputs_wide + branch
    normed_two, norm_two_back = jax.vjp(layer_norm, middle, norm_gain[1], norm_shift[1])
    rounded_two = normed_two.astype(BF)
    hidden = jnp.dot(rounded_two, up_full, preferred_element_type=F32) + up_shift
    activated, gelu_back = jax.vjp(exact_gelu, hidden)
    activated_low = activated.astype(BF)
    block_out = (
        middle + head_total(dot_f32(activated_low, down_full, ((1,), (1,)))) + out_shift[1]
    )
    block_out = block_out.astype(BF).reshape(clip_count, rows_clip, model_width)

    cotan_low = cotangent.reshape(row_total, model_width)
    cotan_wide = cotan_low.astype(F32)
    active_grad = jnp.dot(cotan_low, down_full, preferred_element_type=F32)
    hidden_grad = gelu_back(active_grad)[0].astype(BF)
    grad_up_bias = jnp.sum(hidden_grad.astype(F32), axis=0)
    normed_two_grad = head_total(dot_f32(hidden_grad, up_full, ((1,), (1,))))
    middle_norm_grad, gain_two_grad, shift_two_grad = norm_two_back(normed_two_grad)
    middle_grad = cotan_wide + middle_norm_grad
    branch_grad = middle_grad.astype(BF)
    attended_grad = jnp.dot(branch_grad, proj_full, preferred_element_type=F32).astype(BF)
    attended_grad = attended_grad.reshape(clip_count, rows_clip, head_width)
    attended_grad_own, attended_grad_send = split_groups(attended_grad, which, 2)
    attended_grad_peer = swap(attended_grad_send, "frame")
    backward = attention_backward(
        which_row, joined_own, joined_peer, attended_grad_own, attended_grad_peer, consts, taps,
        gains, bias, saved, scale, unit,
    )
    grad_own, grad_send, mem_grad_own, mem_grad_send = backward[:4]
    taps_grad, pool_gain_grad, pool_shift_grad, bias_grad = backward[4:]
    grad_peer = swap(grad_send, "frame")
    mem_grad_peer = swap(mem_grad_send[:, :CELLS], "frame")

    grad_rest = jnp.concatenate(
        [
            dot_f32(branch_grad, attended, ((0,), (0,))).astype(BF),
            dot_f32(rounded_two, hidden_grad, ((0,), (0,))).astype(BF),
            dot_f32(cotan_low, activated_low, ((0,), (0,))).astype(BF),
        ],
        axis=1,
    )
    rest_shard = lax.psum_scatter(grad_rest, both, scatter_dimension=0, tiled=True).astype(F32)

    def lanes_back(rows, lead):
        return rows.reshape(lead + (-1, heads, LANES))[..., :unit]

    mem_grads = [
        part.reshape(clip_count, CELLS, 2, heads, LANES)[..., :unit]
        for part in (mem_grad_own[:, :CELLS], mem_grad_peer)
    ]
    squeezed_grads = join_groups(mem_grads[0], mem_grads[1], which, 3).astype(F32)
    grad_squeeze = precise("cjsxnd,csxnd->xjd", cached_wide, squeezed_grads)
    time_count = time_rows.shape[1]
    time_grad_rows = bias_grad[:, :time_count, :unit]
    grad_time = precise(
        "ckr,ckd->rd", time_hot.reshape(clip_count, time_count, -1), time_grad_rows
    )
    space_grad_rows = jnp.sum(bias_grad[:, SPACE_AT : SPACE_AT + 2 * CELLS, :unit], axis=0)
    grad_space = precise("pr,xpd->xrd", space_hot, space_grad_rows.reshape(2, CELLS, unit))
    grad_kernel = jnp.sum(lanes_back(jnp.sum(taps_grad, axis=1), (27,)), axis=2).transpose(1, 0, 2)
    grad_pool_gain = jnp.sum(lanes_back(pool_gain_grad, ()), axis=1)
    grad_pool_shift = jnp.sum(lanes_back(pool_shift_grad, ()), axis=1)

    parts = [
        part.reshape(row_total, 3, group_width)
        for part in (grad_own, grad_peer)
    ]
    joined_grad = join_groups(parts[0], parts[1], which, 2).reshape(row_total, 3 * head_width)
    grad_qkv_bias = jnp.sum(joined_grad.astype(F32), axis=0)
    grad_qkv = dot_f32(rounded_one, joined_grad, ((0,), (0,))).astype(BF)
    qkv_shard = lax.psum_scatter(grad_qkv, both, scatter_dimension=0, tiled=True).astype(F32)
    attn_flat = attn_full.reshape(model_width, 3 * head_width)
    normed_one_grad = head_total(dot_f32(joined_grad, attn_flat, ((1,), (1,))))
    input_norm_grad, gain_one_grad, shift_one_grad = norm_one_back(normed_one_grad)
    grad_in = (
        (middle_grad + input_norm_grad).astype(BF).reshape(clip_count, rows_clip, model_width)
    )

    head_index = lax.axis_index("head")
    head_axis = lax.axis_size("head")
    once = (head_index == 0).astype(F32)
    slot = (jnp.arange(head_axis) == head_index).astype(F32)[:, None]
    pieces = [
        jnp.stack([gain_one_grad, gain_two_grad]) * once,
        jnp.stack([shift_one_grad, shift_two_grad]) * once,
        jnp.stack([jnp.sum(middle_grad, axis=0), jnp.sum(cotan_wide, axis=0)]) * once,
        slot * grad_qkv_bias[None],
        slot * grad_up_bias[None],
        grad_kernel,
        grad_pool_gain,
        grad_pool_shift,
        grad_squeeze,
        grad_time,
        grad_space,
    ]
    flat = jnp.concatenate([piece.reshape(-1) for piece in pieces])
    flat = lax.psum(flat, ("clip", "frame", "head"))
    sums = []
    at = 0
    for piece in pieces:
        sums.append(flat[at : at + piece.size].reshape(piece.shape))
        at += piece.size
    gain_sums, shift_sums, out_sums, qkv_bias_sum, up_bias_sum = sums[:5]
    kernel_sum, pool_gain_sum, pool_shift_sum, squeeze_sum, time_sum, space_sum = sums[5:]
    qkv_bias_sum = lax.dynamic_index_in_dim(qkv_bias_sum, head_index, 0, keepdims=False)
    up_bias_sum = lax.dynamic_index_in_dim(up_bias_sum, head_index, 0, keepdims=False)
    return (
        block_out,
        grad_in,
        gain_sums,
        shift_sums,
        qkv_shard.reshape(-1, 3, head_width),
        qkv_bias_sum.reshape(3, head_width),
        kernel_sum,
        pool_gain_sum,
        pool_shift_sum,
        squeeze_sum,
        time_sum,
        space_sum,
        rest_shard[:, :head_width].T,
        out_sums,
        rest_shard[:, head_width : head_width + hidden_width],
        up_bias_sum,
        rest_shard[:, head_width + hidden_width :].T,
    )


def solution(mesh):
    return jax.shard_map(
        local,
        mesh=mesh,
        in_specs=(
            P("clip", "frame", None),
            P("clip", "frame", None, "head"),
            P("clip", "frame", None, "head"),
            P("clip"),
            P("clip", None),
            P(),
            P(),
            P(("clip", "frame"), None, "head"),
            P(None, "head"),
            P(),
            P(),
            P(),
            P(),
            P(),
            P(),
            P("head", ("clip", "frame")),
            P(),
            P(("clip", "frame"), "head"),
            P("head"),
            P("head", ("clip", "frame")),
            P("clip", "frame", None),
        ),
        out_specs=(
            P("clip", "frame", None),
            P("clip", "frame", None),
            P(),
            P(),
            P(("clip", "frame"), None, "head"),
            P(None, "head"),
            P(),
            P(),
            P(),
            P(),
            P(),
            P(),
            P("head", ("clip", "frame")),
            P(),
            P(("clip", "frame"), "head"),
            P("head"),
            P("head", ("clip", "frame")),
        ),
        check_vma=False,
    )
```

time: 2560 us -> 828 us (0.32)
  other arithmetic: 799 us -> 51.7 us
  local copies, waits for them, and re-layouts: 707 us -> 91.9 us
  waiting for transfers between devices: 658 us -> 457 us
  blocking collectives: 173 us -> 0 us
  Pallas kernels: 0 us -> 124 us
  matrix products: 185 us -> 66.6 us
    reduce_sum x6, other arithmetic: 411 us -> 4.78 us  [the longest x1 1.26 us: local(): jnp.sum(taps_grad, axis=1)]
    reshape x13 -> x34, local copies, waits for them, and re-layouts: 311 us -> 28.9 us  [the longest x1 5.09 us: local(): cached_kv.astype(F32)]
    add x3 -> x2, local copies, waits for them, and re-layouts: 238 us -> 0.84 us  [project(): jnp.dot(rounded_one, flat, preferred_element_type=F32) + shift.reshape(-1)]
    reduce_scatter x4 -> x2, waiting for transfers between devices: 474 us -> 263 us  [the longest x1 144 us: local(): lax.psum_scatter(grad_rest, both, scatter_dimension=0, tiled=True)]
    pallas_call x0 -> x2, Pallas kernels: none -> 124 us  [the longest x1 73.4 us: attention_backward(): pl.pallas_call(partial(backward_kernel, heads=heads, unit=unit, scale=sca...]
    psum x2 -> x0, blocking collectives: 121 us -> none  [the longest x1 76.8 us: local(): lax.psum((jnp.stack([gain_one_grad, gain_two_grad]), jnp.stack([shift_one...]
    dot_general x33 -> x17, matrix products: 185 us -> 66.6 us  [the longest x8 29.3 us: dot_f32(): return lax.dot_general(a, b, (dims, ((), ())), preferred_element_type=F32)]
    all_gather x4 -> x2, waiting for transfers between devices: 154 us -> 38 us  [the longest x1 38 us: local(): attn_full = lax.all_gather(qkv_weight, both, axis=0, tiled=True)]
  transfers between devices with their start and end apart: 17 -> 15, of which waited for: 11 -> 10; matrix products, arithmetic and copies ran while one was open for 36% -> 18% of each run, Pallas kernels for 0% -> 6%
where the time goes in v1:
time: 828 us; the launch traced here: 817 us
  waiting for transfers between devices  457 us (55%)
  Pallas kernels  124 us (15%)
  local copies, waits for them, and re-layouts  91.9 us (11%)
  matrix products  66.6 us (8%)
  other arithmetic  51.7 us (6%)
  between operations  15.3 us (2%)
  starting transfers between devices  10.9 us (1%)
    reduce_scatter x1, waiting for transfers between devices, local(): lax.psum_scatter(grad_rest, both, scatter_dimension=0, tiled=True)  144 us
    reduce_scatter x1, waiting for transfers between devices, local(): lax.psum_scatter(grad_qkv, both, scatter_dimension=0, tiled=True)  119 us
    psum x1, waiting for transfers between devices, local(): flat = lax.psum(flat, ('clip', 'frame', 'head'))  92.3 us
    pallas_call x1, Pallas kernels, attention_backward(): pl.pallas_call(partial(backward_kernel, heads=heads, unit=unit, scale=sca...  73.4 us
    ppermute x10, waiting for transfers between devices, swap(): return lax.ppermute(value, axis, [(0, 1), (1, 0)])  62.7 us
    pallas_call x1, Pallas kernels, attention_forward(): pl.pallas_call(partial(forward_kernel, heads=heads, unit=unit, scale=scal...  51 us
    all_gather x1, waiting for transfers between devices, local(): attn_full = lax.all_gather(qkv_weight, both, axis=0, tiled=True)  38 us
    dot_general x8, matrix products, dot_f32(): return lax.dot_general(a, b, (dims, ((), ())), preferred_element_type=F32)  29.3 us
  transfers between devices with their start and end apart: 15, of which 10 were waited for; matrix products, arithmetic and copies ran while one was open for 18% of the time, Pallas kernels for 6%

profile of v1, /device:TPU:0, one launch (start us, length us, event | category | flops | bytes accessed | tf_op | source)
XLA Modules:
  0.0 817.5 jit_solution(381757195992722341)
XLA Ops:
  10.5 5.1 reshape.537
  34.3 38.0 %all-gather.3.cloned.1.call-done = bf16[768,3,384]{2,0,1:T(8,128)(2,1)} async-done(((bf16[48,3,384]{2,0,1:T(8,128)(2,1)}), bf16[768,3,384]{2,0,1:T(8,128)(2,1)}) %all-gather.3.cloned.1.call-update) | async-done | bytes 1769488 | tf_op jit(solution)/shard_map/all_gather | solution.py:571
  75.0 3.5 add_convert_fusion.4
  93.3 3.5 add_convert_fusion.5
  100.5 17.7 %collective-permute-done.peer_ref = bf16[5,196,576]{2,1,0:T(8,128)(2,1)S(1)} collective-permute-done((bf16[5,196,576]{2,1,0:T(8,128)(2,1)}, bf16[5,196,576]{2,1,0:T(8,128)(2,1)S(1)}, u32[]{:S(2)}, u32[]{:S(2)}) %collective-permute-start) | collective-permute-done | bytes 1128992 | tf_op jit(solution)/shard_map/ppermute | solution.py:470
  119.4 51.0 %pooled_attention_forward.1 = (bf16[5,196,192]{2,1,0:T(8,128)(2,1)}, bf16[5,196,192]{2,1,0:T(8,128)(2,1)}, bf16[5,416,256]{2,1,0:T(8,128)(2,1)}, bf16[5,640,256]...) custom-call(s32[1]{0:T(128)} %bitcast.4.which, ...), custom_call_target="tpu_custom_call" | custom-call | tf_op jit(solution)/shard_map/pooled_attention_forward/pallas_call | solution.py:344
  171.9 11.3 %collective-permute-done.2 = bf16[5,196,192]{2,1,0:T(8,128)(2,1)S(1)} collective-permute-done((bf16[5,196,192]{2,1,0:T(8,128)(2,1)}, bf16[5,196,192]{2,1,0:T(8,128)(2,1)S(1)}, u32[]{:S(2)}, u32[]{:S(2)}) %collective-permute-start.2) | collective-permute-done | bytes 376352 | tf_op jit(solution)/shard_map/ppermute | solution.py:470
  184.7 3.4 convolution_convert_fusion.3
  197.4 17.5 %multiply_convert_fusion = (bf16[980,1536]{1,0:T(8,128)(2,1)S(1)}, f32[980,1536]{1,0:T(8,128)S(1)}, f32[980,1536]{1,0:T(8,128)}) fusion(f32[1536]{0:T(1024)S(1)} %copy-done.53, bf16[768,3456]{1,0:T(8,128)(2,1)S(1)} %bitcast.117, f32[980,768]{1,0:T(8,128)S(1)} %get-tuple-element.143, f32[768]{0:T(1024)S(1)} %copy-done.47, f32[768]{0:T(1024)S(1)} %copy-done.30, ...), kind=kOutput, calls=%fused_computation.14 | convolution fusion | flops 2415221760 | bytes 20459520 | tf_op jit(solution)/shard_map/dot_general | solution.py:627
  214.9 8.2 %convert_reduce_fusion = (f32[1536]{0:T(1024)S(1)}, bf16[980,1536]{1,0:T(8,128)(2,1)S(1)}) fusion(f32[980,1536]{1,0:T(8,128)S(1)} %get-tuple-element.141, bf16[980,768]{1,0:T(8,128)(2,1)S(1)} %copy-done.11, bf16[768,3456]{1,0:T(8,128)(2,1)S(1)} %bitcast.117, f32[980,1536]{1,0:T(8,128)} %get-tuple-element.168, f32[1536]{0:T(1024)S(1)} %copy-done.53), kind=kOutput, calls=%fused_computation.13 | convolution fusion | flops 2337698304 | bytes 18962432 | tf_op jit(solution)/shard_map/dot_general | solution.py:637
  245.4 12.1 %collective-permute-done.6.grad_peer_ref = bf16[5,196,192]{2,1,0:T(8,128)(2,1)} collective-permute-done((bf16[5,196,192]{2,1,0:T(8,128)(2,1)}, bf16[5,196,192]{2,1,0:T(8,128)(2,1)}, u32[]{:S(2)}, u32[]{:S(2)}) %collective-permute-start.6) | collective-permute-done | bytes 376352 | tf_op jit(solution)/shard_map/ppermute | solution.py:470
  257.5 73.4 %pooled_attention_backward.1 = (bf16[5,196,576]{2,1,0:T(8,128)(2,1)}, bf16[5,196,576]{2,1,0:T(8,128)(2,1)}, bf16[5,112,512]{2,1,0:T(8,128)(2,1)}, bf16[5,112,512...) custom-call(s32[1]{0:T(128)} %bitcast.4.which, ...), custom_call_target="tpu_custom_call" | custom-call | tf_op jit(solution)/shard_map/pooled_attention_backward/pallas_call | solution.py:401
  342.7 19.7 %collective-permute-done.7 = bf16[5,196,576]{2,1,0:T(8,128)(2,1)} collective-permute-done((bf16[5,196,576]{2,1,0:T(8,128)(2,1)}, bf16[5,196,576]{2,1,0:T(8,128)(2,1)}, u32[]{:S(2)}, u32[]{:S(2)}) %collective-permute-start.7) | collective-permute-done | bytes 1128992 | tf_op jit(solution)/shard_map/ppermute | solution.py:470
  362.4 3.4 broadcast_select_fusion.1
  365.8 4.6 select_n.130
  373.3 4.9 select_n.132
  393.7 4.2 copy.88
  407.8 4.9 convolution_convert_fusion.2
  412.8 6.5 fusion.13
  419.3 4.2 convolution_convert_fusion.1
  426.8 4.5 pad_maximum_fusion
  436.1 92.3 %all-reduce.6.cloned.1.call-done = f32[43968]{0:T(1024)} async-done(((f32[43968]{0:T(1024)}), f32[43968]{0:T(1024)}) %all-reduce.6.cloned.1.call-update) | async-done | bytes 175888 | tf_op jit(solution)/shard_map/psum | solution.py:720
  541.9 119.3 %reduce-scatter.3.cloned.1.call-done = bf16[48,1152]{1,0:T(8,128)(2,1)} async-done(((bf16[768,1152]{1,0:T(8,128)(2,1)}), bf16[48,1152]{1,0:T(8,128)(2,1)}) %reduce-scatter.3.cloned.1.call-update) | async-done | bytes 110608 | tf_op jit(solution)/shard_map/reduce_scatter | solution.py:694
  662.8 143.6 %reduce-scatter.5.cloned.1.call-done = bf16[48,3456]{1,0:T(8,128)(2,1)} async-done(((bf16[768,3456]{1,0:T(8,128)(2,1)}), bf16[48,3456]{1,0:T(8,128)(2,1)}) %reduce-scatter.5.cloned.1.call-update) | async-done | bytes 331792 | tf_op jit(solution)/shard_map/reduce_scatter | solution.py:665
  (314 shorter events, 145.5 us)
Async XLA Ops:
  7.2 76.6 %copy-start = (f32[233,96]{0,1:T(8,128)S(1)}, f32[233,96]{0,1:T(8,128)}, u32[]{:S(2)}) copy-start(f32[233,96]{0,1:T(8,128)} %param.48) | copy-start | bytes 268420
  7.2 65.1 %all-gather.3.cloned.1.call-start = ((), (), s32[]{:S(2)}) async-start(), calls=%async_computation.2 | async-start | bytes 1880064 | tf_op jit(solution)/shard_map/all_gather | solution.py:571
  7.9 176.8 %all-gather.5.cloned.1.call-start = ((), (), s32[]{:S(2)}) async-start(), calls=%async_computation.3 | async-start | bytes 5640192 | tf_op jit(solution)/shard_map/all_gather | solution.py:573
  9.8 518.6 %all-reduce.6.cloned.1.call-start = ((), (), s32[]{:S(2)}) async-start(), calls=%async_computation.4 | async-start | bytes 352256 | tf_op jit(solution)/shard_map/psum | solution.py:720
  18.5 10.7 %copy-start.45 = (f32[2,768]{1,0:T(2,128)S(1)}, f32[2,768]{1,0:T(2,128)}, u32[]{:S(2)}) copy-start(f32[2,768]{1,0:T(2,128)} %param.41) | copy-start | bytes 18436
  18.5 11.3 %copy-start.4 = (bf16[5,196,768]{2,1,0:T(8,128)(2,1)S(1)}, bf16[5,196,768]{2,1,0:T(8,128)(2,1)}, u32[]{:S(2)}) copy-start(bf16[5,196,768]{2,1,0:T(8,128)(2,1)} %param.35) | copy-start | bytes 4515844
  23.4 77.2 %collective-permute-start.1 = (bf16[5,98,384]{2,1,0:T(8,128)(2,1)}, bf16[5,98,384]{2,1,0:T(8,128)(2,1)}, u32[]{:S(2)}, u32[]{:S(2)}) collective-permute-start(bf16[5,98,384]{2,1,0:T(8,128)(2,1)} %reshape.540), channel_id=1, source_target_pairs={{0,2},{2,0},{1,3},{3,1},{4,6},{6,4},{5,7},{7,5},{8,10},{10,8},{9,1... | collective-permute-start | bytes 1128968 | tf_op jit(solution)/shard_map/ppermute | solution.py:470
  82.3 35.9 %collective-permute-start = (bf16[5,196,576]{2,1,0:T(8,128)(2,1)}, bf16[5,196,576]{2,1,0:T(8,128)(2,1)S(1)}, u32[]{:S(2)}, u32[]{:S(2)}) collective-permute-start(bf16[5,196,576]{2,1,0:T(8,128)(2,1)} %reshape.536), channel_id=1, source_target_pairs={{0,2},{2,0},{1,3},{3,1},{4,6},{6,4},{5,7},{7,5},{8,10},{10,8},{9,1... | collective-permute-start | bytes 3386888 | tf_op jit(solution)/shard_map/ppermute | solution.py:470
  170.4 12.8 %collective-permute-start.2 = (bf16[5,196,192]{2,1,0:T(8,128)(2,1)}, bf16[5,196,192]{2,1,0:T(8,128)(2,1)S(1)}, u32[]{:S(2)}, u32[]{:S(2)}) collective-permute-start(bf16[5,196,192]{2,1,0:T(8,128)(2,1)} %get-tuple-element.57), channel_id=1, source_target_pairs={{0,2},{2,0},{1,3},{3,1},{4,6},{6,4},{5,7},{7,5},{8,10},{10,8},{9,1... | collective-permute-start | bytes 1128968 | tf_op jit(solution)/shard_map/ppermute | solution.py:470
  188.2 5.5 collective-permute-start.3
  196.3 35.9 %copy-start.2 = (f32[980,768]{1,0:T(8,128)}, f32[980,768]{1,0:T(8,128)S(1)}, u32[]{:S(2)}) copy-start(f32[980,768]{1,0:T(8,128)S(1)} %get-tuple-element.143) | copy-start | bytes 9031684
  196.9 35.3 %copy-start.32 = (f32[980]{0:T(1024)}, f32[980]{0:T(1024)S(1)}, u32[]{:S(2)}) copy-start(f32[980]{0:T(1024)S(1)} %fusion.40) | copy-start | bytes 11764
  197.4 17.5 %copy-start.11 = (bf16[980,768]{1,0:T(8,128)(2,1)S(1)}, bf16[980,768]{1,0:T(8,128)(2,1)}, u32[]{:S(2)}) copy-start(bf16[980,768]{1,0:T(8,128)(2,1)} %reshape.545) | copy-start | bytes 4515844
  214.9 11.4 %copy-start.55 = (bf16[980,1536]{1,0:T(8,128)(2,1)}, bf16[980,1536]{1,0:T(8,128)(2,1)S(1)}, u32[]{:S(2)}) copy-start(bf16[980,1536]{1,0:T(8,128)(2,1)S(1)} %get-tuple-element.140) | copy-start | bytes 9031684
  225.7 3.5 collective-permute-start.5
  228.8 3.4 collective-permute-start.4
  243.5 14.0 %collective-permute-start.6 = (bf16[5,196,192]{2,1,0:T(8,128)(2,1)}, bf16[5,196,192]{2,1,0:T(8,128)(2,1)}, u32[]{:S(2)}, u32[]{:S(2)}) collective-permute-start(bf16[5,196,192]{2,1,0:T(8,128)(2,1)} %get-tuple-element.153), channel_id=1, source_target_pairs={{0,2},{2,0},{1,3},{3,1},{4,6},{6,4},{5,7},{7,5},{8,10},{10,8},{9,1... | collective-permute-start | bytes 1128968 | tf_op jit(solution)/shard_map/ppermute | solution.py:470
  257.5 76.9 %copy-start.36 = (f32[5,196]{1,0:T(8,128)S(1)}, f32[5,196]{1,0:T(8,128)}, u32[]{:S(2)}) copy-start(f32[5,196]{1,0:T(8,128)} %get-tuple-element.164) | copy-start | bytes 11764
  330.9 31.4 %collective-permute-start.7 = (bf16[5,196,576]{2,1,0:T(8,128)(2,1)}, bf16[5,196,576]{2,1,0:T(8,128)(2,1)}, u32[]{:S(2)}, u32[]{:S(2)}) collective-permute-start(bf16[5,196,576]{2,1,0:T(8,128)(2,1)} %get-tuple-element.64), channel_id=1, source_target_pairs={{0,2},{2,0},{1,3},{3,1},{4,6},{6,4},{5,7},{7,5},{8,10},{10,8},{9,1... | collective-permute-start | bytes 3386888 | tf_op jit(solution)/shard_map/ppermute | solution.py:470
  342.4 46.4 %collective-permute-start.9 = (bf16[5,49,512]{2,1,0:T(8,128)(2,1)}, bf16[5,49,512]{2,1,0:T(8,128)(2,1)}, u32[]{:S(2)}, u32[]{:S(2)}) collective-permute-start(bf16[5,49,512]{2,1,0:T(8,128)(2,1)} %slice.219), channel_id=1, source_target_pairs={{0,2},{2,0},{1,3},{3,1},{4,6},{6,4},{5,7},{7,5},{8,10},{10,8},{9,1... | collective-permute-start | bytes 752648 | tf_op jit(solution)/shard_map/ppermute | solution.py:470
  385.0 13.0 %collective-permute-start.8 = (bf16[980,768]{1,0:T(8,128)(2,1)}, bf16[980,768]{1,0:T(8,128)(2,1)}, u32[]{:S(2)}, u32[]{:S(2)}) collective-permute-start(bf16[980,768]{1,0:T(8,128)(2,1)} %bitcast_convert_fusion), channel_id=1, source_target_pairs={{0,1},{1,0},{2,3},{3,2},{4,5},{5,4},{6,7},{7,6},{8,9},{9,8},{10,11... | collective-permute-start | bytes 4515848 | tf_op jit(solution)/shard_map/ppermute | solution.py:470
  407.4 253.8 %reduce-scatter.3.cloned.1.call-start = ((), (), s32[]{:S(2)}) async-start(), calls=%async_computation.5 | async-start | bytes 1880064 | tf_op jit(solution)/shard_map/reduce_scatter | solution.py:694
  412.7 393.7 %reduce-scatter.5.cloned.1.call-start = ((), (), s32[]{:S(2)}) async-start(), calls=%async_computation.6 | async-start | bytes 5640192 | tf_op jit(solution)/shard_map/reduce_scatter | solution.py:665
  434.4 376.1 %copy-start.1 = (f32[233,96]{0,1:T(8,128)S(1)}, f32[233,96]{0,1:T(8,128)}, u32[]{:S(2)}) copy-start(f32[233,96]{0,1:T(8,128)} %param.48) | copy-start | bytes 268420
  (51 other events, 213.6 us)
Sparse Core Ops, SparseCore 0:
  10.7 61.5 all-gather.2
  75.1 87.6 all-gather.4
  407.5 120.7 all-reduce.5
  533.1 128.1 reduce-scatter.2
  666.3 140.0 reduce-scatter.4

commit v2 on v1

--- a/solution.py
+++ b/solution.py
@@ -25,6 +25,7 @@
 BF = jnp.bfloat16
 F32 = jnp.float32
 VMEM_LIMIT = 60 * 1024 * 1024
+MESH_ID = pl.DeviceIdType.MESH
 
 
 def dot_f32(a, b, dims):
@@ -455,6 +456,170 @@
     )(which, own, peer, grad_own, grad_peer, into, outof, taps, gains, bias, keyhot, mask, *saved)
 
 
+def device_of(outer, inner, frame, head):
+    return (outer * 2 + inner, frame, head)
+
+
+def plane_peer(inner, frame, step):
+    return (inner + step // 2) % 2, (frame + step % 2) % 2
+
+
+def finish_kernel(
+    grads, small, out, small_out, near, part, far, small_in,
+    near_send, near_recv, far_send, far_recv, first_send, first_recv, second_send, second_recv,
+):
+    outers, shard_rows, width = part.shape[1], part.shape[2], grads.shape[3]
+    chunks = part.shape[0]
+    cols = width // chunks
+    devices = small.shape[0]
+    clip = lax.axis_index("clip")
+    frame = lax.axis_index("frame")
+    head = lax.axis_index("head")
+    outer, inner = clip // 2, clip % 2
+    place = inner * 2 + frame
+    mine = (clip * 2 + frame) * 2 + head
+
+    def device(index):
+        return (index // 4, (index // 2) % 2, index % 2)
+
+    barrier = pltpu.get_barrier_semaphore()
+
+    def greet(step, carry):
+        pl.semaphore_signal(
+            barrier, inc=1, device_id=device((mine + step) % devices), device_id_type=MESH_ID
+        )
+        return carry
+
+    lax.fori_loop(1, devices, greet, 0)
+    pl.semaphore_wait(barrier, devices - 1)
+
+    def first(step):
+        other = (mine + step) % devices
+        return pltpu.make_async_remote_copy(
+            src_ref=small.at[other], dst_ref=small_in.at[step],
+            send_sem=first_send.at[step], recv_sem=first_recv.at[step],
+            device_id=device(other), device_id_type=MESH_ID,
+        )
+
+    def second(step):
+        return pltpu.make_async_remote_copy(
+            src_ref=small_out.at[mine], dst_ref=small_out.at[mine],
+            send_sem=second_send.at[step], recv_sem=second_recv.at[step],
+            device_id=device((mine + step) % devices), device_id_type=MESH_ID,
+        )
+
+    def second_in(step):
+        other = (mine + devices - step) % devices
+        return pltpu.make_async_remote_copy(
+            src_ref=small_out.at[other], dst_ref=small_out.at[other],
+            send_sem=second_send.at[step], recv_sem=second_recv.at[step],
+            device_id=device((mine + step) % devices), device_id_type=MESH_ID,
+        )
+
+    def near_copy(chunk, step):
+        there_inner, there_frame = plane_peer(inner, frame, step)
+        return pltpu.make_async_remote_copy(
+            src_ref=grads.at[:, there_inner * 2 + there_frame, :, pl.ds(chunk * cols, cols)],
+            dst_ref=near.at[chunk, step - 1],
+            send_sem=near_send.at[chunk, step - 1], recv_sem=near_recv.at[chunk, step - 1],
+            device_id=device_of(outer, there_inner, there_frame, head), device_id_type=MESH_ID,
+        )
+
+    def far_copy(chunk, step):
+        there = (outer + step) % outers
+        return pltpu.make_async_remote_copy(
+            src_ref=part.at[chunk, there], dst_ref=far.at[chunk, step],
+            send_sem=far_send.at[chunk, step], recv_sem=far_recv.at[chunk, step],
+            device_id=device_of(there, inner, frame, head), device_id_type=MESH_ID,
+        )
+
+    def each(low, high, act):
+        def body(step, carry):
+            act(step)
+            return carry
+
+        lax.fori_loop(low, high, body, 0)
+
+    each(1, devices, lambda step: first(step).start())
+    for chunk in range(chunks):
+        for step in range(1, 4):
+            near_copy(chunk, step).start()
+
+    each(1, devices, lambda step: first(step).wait_recv())
+    total = lax.fori_loop(
+        1, devices, lambda step, total: total + small_in[step], small[mine]
+    )
+    small_out[mine] = total
+    each(1, devices, lambda step: second(step).start())
+
+    for chunk in range(chunks):
+        lanes = slice(chunk * cols, (chunk + 1) * cols)
+        for step in range(1, 4):
+            near_copy(chunk, step).wait_recv()
+
+        def gathered(index):
+            value = grads[index, place, :, lanes].astype(F32)
+            for step in range(3):
+                value = value + near[chunk, step, index].astype(F32)
+            return value
+
+        def send(step):
+            there = (outer + step) % outers
+            part[chunk, there] = gathered(there).astype(BF)
+            far_copy(chunk, step).start()
+
+        each(1, outers, send)
+        out[:, lanes] = gathered(outer)
+    for chunk in range(chunks):
+        lanes = slice(chunk * cols, (chunk + 1) * cols)
+        each(1, outers, lambda step: far_copy(chunk, step).wait_recv())
+        out[:, lanes] = lax.fori_loop(
+            1, outers, lambda step, total: total + far[chunk, step].astype(F32), out[:, lanes]
+        )
+    each(1, devices, lambda step: second_in(step).wait_recv())
+    each(1, devices, lambda step: first(step).wait_send())
+    each(1, devices, lambda step: second(step).wait_send())
+    for chunk in range(chunks):
+        for step in range(1, 4):
+            near_copy(chunk, step).wait_send()
+        each(1, outers, lambda step: far_copy(chunk, step).wait_send())
+
+
+def finish(grads, small, clip_count, devices):
+    outers = clip_count // 2
+    shard_rows = grads.shape[0] // (4 * outers)
+    width = grads.shape[1]
+    chunks = 3
+    cols = width // chunks
+    out = jax.ShapeDtypeStruct
+    dma = pltpu.SemaphoreType.DMA
+    vmem = pl.BlockSpec(memory_space=pltpu.VMEM)
+    return pl.pallas_call(
+        finish_kernel,
+        in_specs=[vmem, vmem],
+        out_specs=[vmem, vmem],
+        out_shape=[out((shard_rows, width), F32), out(small.shape, F32)],
+        scratch_shapes=[
+            pltpu.VMEM((chunks, 3, outers, shard_rows, cols), BF),
+            pltpu.VMEM((chunks, outers, shard_rows, cols), BF),
+            pltpu.VMEM((chunks, outers, shard_rows, cols), BF),
+            pltpu.VMEM(small.shape, F32),
+            dma((chunks, 3)),
+            dma((chunks, 3)),
+            dma((chunks, outers)),
+            dma((chunks, outers)),
+            dma((devices,)),
+            dma((devices,)),
+            dma((devices,)),
+            dma((devices,)),
+        ],
+        compiler_params=pltpu.CompilerParams(
+            collective_id=0, has_side_effects=True, vmem_limit_bytes=VMEM_LIMIT
+        ),
+        name="finish_reductions",
+    )(grads.reshape(outers, 4, shard_rows, width), small)
+
+
 def layer_norm(values, gain_row, shift_row):
     average = jnp.mean(values, axis=-1, keepdims=True)
     centred = values - average
@@ -643,17 +808,6 @@
     branch_grad = middle_grad.astype(BF)
     attended_grad = jnp.dot(branch_grad, proj_full, preferred_element_type=F32).astype(BF)
     attended_grad = attended_grad.reshape(clip_count, rows_clip, head_width)
-    attended_grad_own, attended_grad_send = split_groups(attended_grad, which, 2)
-    attended_grad_peer = swap(attended_grad_send, "frame")
-    backward = attention_backward(
-        which_row, joined_own, joined_peer, attended_grad_own, attended_grad_peer, consts, taps,
-        gains, bias, saved, scale, unit,
-    )
-    grad_own, grad_send, mem_grad_own, mem_grad_send = backward[:4]
-    taps_grad, pool_gain_grad, pool_shift_grad, bias_grad = backward[4:]
-    grad_peer = swap(grad_send, "frame")
-    mem_grad_peer = swap(mem_grad_send[:, :CELLS], "frame")
-
     grad_rest = jnp.concatenate(
         [
             dot_f32(branch_grad, attended, ((0,), (0,))).astype(BF),
@@ -662,7 +816,19 @@
         ],
         axis=1,
     )
+    grad_rest, attended_grad = lax.optimization_barrier((grad_rest, attended_grad))
     rest_shard = lax.psum_scatter(grad_rest, both, scatter_dimension=0, tiled=True).astype(F32)
+
+    attended_grad_own, attended_grad_send = split_groups(attended_grad, which, 2)
+    attended_grad_peer = swap(attended_grad_send, "frame")
+    backward = attention_backward(
+        which_row, joined_own, joined_peer, attended_grad_own, attended_grad_peer, consts, taps,
+        gains, bias, saved, scale, unit,
+    )
+    grad_own, grad_send, mem_grad_own, mem_grad_send = backward[:4]
+    taps_grad, pool_gain_grad, pool_shift_grad, bias_grad = backward[4:]
+    grad_peer = swap(grad_send, "frame")
+    mem_grad_peer = swap(mem_grad_send[:, :CELLS], "frame")
 
     def lanes_back(rows, lead):
         return rows.reshape(lead + (-1, heads, LANES))[..., :unit]
@@ -691,7 +857,6 @@
     joined_grad = join_groups(parts[0], parts[1], which, 2).reshape(row_total, 3 * head_width)
     grad_qkv_bias = jnp.sum(joined_grad.astype(F32), axis=0)
     grad_qkv = dot_f32(rounded_one, joined_grad, ((0,), (0,))).astype(BF)
-    qkv_shard = lax.psum_scatter(grad_qkv, both, scatter_dimension=0, tiled=True).astype(F32)
     attn_flat = attn_full.reshape(model_width, 3 * head_width)
     normed_one_grad = head_total(dot_f32(joined_grad, attn_flat, ((1,), (1,))))
     input_norm_grad, gain_one_grad, shift_one_grad = norm_one_back(normed_one_grad)
@@ -717,7 +882,13 @@
         grad_space,
     ]
     flat = jnp.concatenate([piece.reshape(-1) for piece in pieces])
-    flat = lax.psum(flat, ("clip", "frame", "head"))
+    devices = lax.axis_size("clip") * frame_count * head_axis
+    block = -(-flat.size // (devices * 8 * LANES)) * 8
+    flat = jnp.pad(flat, (0, devices * block * LANES - flat.size))
+    qkv_shard, flat = finish(
+        grad_qkv, flat.reshape(devices, block, LANES), lax.axis_size("clip"), devices
+    )
+    flat = flat.reshape(-1)
     sums = []
     at = 0
     for piece in pieces:

time: 828 us -> 522 us (0.63)
  waiting for transfers between devices: 457 us -> 115 us
  Pallas kernels: 124 us -> 164 us
    reduce_scatter x1, waiting for transfers between devices: 144 us -> 0.01 us  [local(): lax.psum_scatter(grad_rest, both, scatter_dimension=0, tiled=True)]
    reduce_scatter x1 -> x0, waiting for transfers between devices: 119 us -> none  [local(): lax.psum_scatter(grad_qkv, both, scatter_dimension=0, tiled=True)]
    psum x1 -> x0, waiting for transfers between devices: 92.3 us -> none  [local(): flat = lax.psum(flat, ('clip', 'frame', 'head'))]
    pallas_call x0 -> x1, Pallas kernels: none -> 39.5 us  [finish(): pl.pallas_call(finish_kernel, in_specs=[vmem, vmem], out_specs=[vmem, vme...]
    ppermute x10, waiting for transfers between devices: 62.7 us -> 75.9 us  [swap(): return lax.ppermute(value, axis, [(0, 1), (1, 0)])]
  transfers between devices with their start and end apart: 15 -> 13, of which waited for: 10 -> 5; matrix products, arithmetic and copies ran while one was open for 18% -> 28% of each run, Pallas kernels for 6% -> 32%
where the time goes in v2:
time: 522 us; the launch traced here: 512 us
  Pallas kernels  164 us (31%)
  waiting for transfers between devices  115 us (22%)
  local copies, waits for them, and re-layouts  92.5 us (18%)
  matrix products  66.2 us (13%)
  other arithmetic  48.4 us (9%)
  between operations  15.1 us (3%)
  starting transfers between devices  10.6 us (2%)
    ppermute x10, waiting for transfers between devices, swap(): return lax.ppermute(value, axis, [(0, 1), (1, 0)])  75.9 us
    pallas_call x1, Pallas kernels, attention_backward(): pl.pallas_call(partial(backward_kernel, heads=heads, unit=unit, scale=sca...  73.6 us
    pallas_call x1, Pallas kernels, attention_forward(): pl.pallas_call(partial(forward_kernel, heads=heads, unit=unit, scale=scal...  51 us
    pallas_call x1, Pallas kernels, finish(): pl.pallas_call(finish_kernel, in_specs=[vmem, vmem], out_specs=[vmem, vme...  39.5 us
    all_gather x1, waiting for transfers between devices, local(): attn_full = lax.all_gather(qkv_weight, both, axis=0, tiled=True)  38 us
    dot_general x8, matrix products, dot_f32(): return lax.dot_general(a, b, (dims, ((), ())), preferred_element_type=F32)  27.7 us
    dot_general x1, matrix products, local(): jnp.dot(rounded_two, up_full, preferred_element_type=F32) + up_shift  17.5 us
    ppermute x10, starting transfers between devices, swap(): return lax.ppermute(value, axis, [(0, 1), (1, 0)])  10.5 us
  transfers between devices with their start and end apart: 13, of which 5 were waited for; matrix products, arithmetic and copies ran while one was open for 28% of the time, Pallas kernels for 32%

profile of v2, /device:TPU:0, one launch (start us, length us, event | category | flops | bytes accessed | tf_op | source)
XLA Modules:
  0.0 511.5 jit_solution(9535891470901639782)
XLA Ops:
  10.5 5.1 reshape.519
  34.3 38.0 %all-gather.3.cloned.1.call-done = bf16[768,3,384]{2,0,1:T(8,128)(2,1)} async-done(((bf16[48,3,384]{2,0,1:T(8,128)(2,1)}), bf16[768,3,384]{2,0,1:T(8,128)(2,1)}) %all-gather.3.cloned.1.call-update) | async-done | bytes 1769488 | tf_op jit(solution)/shard_map/all_gather | solution.py:736
  75.1 3.5 add_convert_fusion.4
  93.3 3.5 add_convert_fusion.5
  100.6 17.7 %collective-permute-done.peer_ref = bf16[5,196,576]{2,1,0:T(8,128)(2,1)S(1)} collective-permute-done((bf16[5,196,576]{2,1,0:T(8,128)(2,1)}, bf16[5,196,576]{2,1,0:T(8,128)(2,1)S(1)}, u32[]{:S(2)}, u32[]{:S(2)}) %collective-permute-start) | collective-permute-done | bytes 1128992 | tf_op jit(solution)/shard_map/ppermute | solution.py:635
  119.5 51.0 %pooled_attention_forward.1 = (bf16[5,196,192]{2,1,0:T(8,128)(2,1)}, bf16[5,196,192]{2,1,0:T(8,128)(2,1)}, bf16[5,416,256]{2,1,0:T(8,128)(2,1)}, bf16[5,640,256]...) custom-call(s32[1]{0:T(128)} %bitcast.4.which, ...), custom_call_target="tpu_custom_call" | custom-call | tf_op jit(solution)/shard_map/pooled_attention_forward/pallas_call | solution.py:345
  172.0 11.3 %collective-permute-done.2 = bf16[5,196,192]{2,1,0:T(8,128)(2,1)S(1)} collective-permute-done((bf16[5,196,192]{2,1,0:T(8,128)(2,1)}, bf16[5,196,192]{2,1,0:T(8,128)(2,1)S(1)}, u32[]{:S(2)}, u32[]{:S(2)}) %collective-permute-start.2) | collective-permute-done | bytes 376352 | tf_op jit(solution)/shard_map/ppermute | solution.py:635
  184.9 3.4 convolution_convert_fusion.3
  197.4 17.5 %multiply_convert_fusion = (bf16[980,1536]{1,0:T(8,128)(2,1)S(1)}, f32[980,1536]{1,0:T(8,128)S(1)}, f32[980,1536]{1,0:T(8,128)}) fusion(f32[1536]{0:T(1024)S(1)} %copy-done.42, bf16[768,3456]{1,0:T(8,128)(2,1)S(1)} %bitcast.130, f32[980,768]{1,0:T(8,128)S(1)} %get-tuple-element.151, f32[768]{0:T(1024)S(1)} %copy-done.35, f32[768]{0:T(1024)S(1)} %copy-done.24, ...), kind=kOutput, calls=%fused_computation.14 | convolution fusion | flops 2415221760 | bytes 20459520 | tf_op jit(solution)/shard_map/dot_general | solution.py:792
  214.9 7.1 %convert_reduce_fusion = (f32[1536]{0:T(1024)S(1)}, bf16[980,1536]{1,0:T(8,128)(2,1)S(1)}) fusion(f32[980,1536]{1,0:T(8,128)S(1)} %get-tuple-element.149, bf16[980,768]{1,0:T(8,128)(2,1)S(1)} %copy-done.8, bf16[768,3456]{1,0:T(8,128)(2,1)S(1)} %bitcast.130, f32[980,1536]{1,0:T(8,128)} %get-tuple-element.176, f32[1536]{0:T(1024)S(1)} %copy-done.42), kind=kOutput, calls=%fused_computation.13 | convolution fusion | flops 2337698304 | bytes 18962432 | tf_op jit(solution)/shard_map/dot_general | solution.py:802
  227.8 4.0 fusion.13
  231.8 4.3 convolution_convert_fusion.2
  246.4 4.4 convolution_convert_fusion.4
  252.8 5.7 %pad_maximum_fusion = bf16[768,3456]{1,0:T(8,128)(2,1)} fusion(bf16[768,1536]{1,0:T(8,128)(2,1)} %fusion.13, bf16[768,1536]{1,0:T(8,128)(2,1)} %convolution_convert_fusion.2, bf16[768,384]{1,0:T(8,128)(2,1)} %copy.84), kind=kLoop, calls=%fused_computation.28 | loop fusion | flops 15925248 | bytes 10616832 | tf_op jit(solution)/shard_map/concatenate | solution.py:811
  264.6 13.0 %collective-permute-done.6.grad_peer_ref = bf16[5,196,192]{2,1,0:T(8,128)(2,1)} collective-permute-done((bf16[5,196,192]{2,1,0:T(8,128)(2,1)}, bf16[5,196,192]{2,1,0:T(8,128)(2,1)}, u32[]{:S(2)}, u32[]{:S(2)}) %collective-permute-start.6) | collective-permute-done | bytes 376352 | tf_op jit(solution)/shard_map/ppermute | solution.py:635
  277.7 73.6 %pooled_attention_backward.1 = (bf16[5,196,576]{2,1,0:T(8,128)(2,1)}, bf16[5,196,576]{2,1,0:T(8,128)(2,1)}, bf16[5,112,512]{2,1,0:T(8,128)(2,1)}, bf16[5,112,512...) custom-call(s32[1]{0:T(128)} %bitcast.4.which, ...), custom_call_target="tpu_custom_call" | custom-call | tf_op jit(solution)/shard_map/pooled_attention_backward/pallas_call | solution.py:402
  365.2 33.8 %collective-permute-done.9 = bf16[5,49,512]{2,1,0:T(8,128)(2,1)} collective-permute-done((bf16[5,49,512]{2,1,0:T(8,128)(2,1)}, bf16[5,49,512]{2,1,0:T(8,128)(2,1)}, u32[]{:S(2)}, u32[]{:S(2)}) %collective-permute-start.9) | collective-permute-done | bytes 250912 | tf_op jit(solution)/shard_map/ppermute | solution.py:635
  400.3 3.4 broadcast_select_fusion.1
  403.8 4.6 select_n.130
  411.3 4.9 select_n.132
  420.5 3.3 bitcast_convert_fusion
  426.8 4.2 copy.87
  431.1 5.6 %convolution_convert_fusion = bf16[768,1152]{1,0:T(8,128)(2,1)} fusion(bf16[980,768]{1,0:T(8,128)(2,1)} %convert_element_type.145, bf16[980,1152]{0,1:T(8,128)(2,1)} %bitcast.100), kind=kOutput, calls=%fused_computation.34 | convolution fusion | flops 1734967296 | bytes 5532672 | tf_op jit(solution)/shard_map/dot_general | solution.py:32
  445.0 39.5 %finish_reductions.1 = (f32[48,1152]{1,0:T(8,128)}, f32[32,16,128]{2,1,0:T(8,128)}) custom-call(bf16[4,4,48,1152]{3,2,1,0:T(8,128)(2,1)} %bitcast.102, f32[32,16,128]{2,1,0:T(8,128)} %bitcast.103), custom_call_target="tpu_custom_call" | custom-call | tf_op jit(solution)/shard_map/finish_reductions/pallas_call | solution.py:597
  (281 shorter events, 134.0 us)
Async XLA Ops:
  7.2 76.7 %copy-start = (f32[233,96]{0,1:T(8,128)S(1)}, f32[233,96]{0,1:T(8,128)}, u32[]{:S(2)}) copy-start(f32[233,96]{0,1:T(8,128)} %param.48) | copy-start | bytes 268420
  7.2 65.1 %all-gather.3.cloned.1.call-start = ((), (), s32[]{:S(2)}) async-start(), calls=%async_computation.1 | async-start | bytes 1880064 | tf_op jit(solution)/shard_map/all_gather | solution.py:736
  7.9 176.9 %all-gather.5.cloned.1.call-start = ((), (), s32[]{:S(2)}) async-start(), calls=%async_computation.2 | async-start | bytes 5640192 | tf_op jit(solution)/shard_map/all_gather | solution.py:738
  9.8 490.8 %reduce-scatter.2.cloned.1.call-start = ((), (), s32[]{:S(2)}) async-start(), calls=%async_computation.3 | async-start | bytes 5640192 | tf_op jit(solution)/shard_map/reduce_scatter | solution.py:820
  10.5 9.3 %copy-start.17 = (bf16[5,49,2,384]{3,2,1,0:T(2,128)(2,1)S(1)}, bf16[5,49,2,384]{3,2,1,0:T(2,128)(2,1)}, u32[]{:S(2)}) copy-start(bf16[5,49,2,384]{3,2,1,0:T(2,128)(2,1)} %param.37) | copy-start | bytes 1128964
  18.5 9.9 %copy-start.25 = (f32[49,13,1]{0,1,2:T(8,128)S(1)}, f32[49,13,1]{0,1,2:T(8,128)}, u32[]{:S(2)}) copy-start(f32[49,13,1]{0,1,2:T(8,128)} %constant.216) | copy-start | bytes 7648
  18.5 9.9 %copy-start.28 = (f32[2,13,96]{2,0,1:T(2,128)S(1)}, f32[2,13,96]{2,0,1:T(2,128)}, u32[]{:S(2)}) copy-start(f32[2,13,96]{2,0,1:T(2,128)} %param.49) | copy-start | bytes 29956
  18.5 10.1 %copy-start.32 = (f32[2,768]{1,0:T(2,128)S(1)}, f32[2,768]{1,0:T(2,128)}, u32[]{:S(2)}) copy-start(f32[2,768]{1,0:T(2,128)} %param.40) | copy-start | bytes 18436
  18.5 10.7 %copy-start.33 = (f32[2,768]{1,0:T(2,128)S(1)}, f32[2,768]{1,0:T(2,128)}, u32[]{:S(2)}) copy-start(f32[2,768]{1,0:T(2,128)} %param.41) | copy-start | bytes 18436
  18.5 11.3 %copy-start.2 = (bf16[5,196,768]{2,1,0:T(8,128)(2,1)S(1)}, bf16[5,196,768]{2,1,0:T(8,128)(2,1)}, u32[]{:S(2)}) copy-start(bf16[5,196,768]{2,1,0:T(8,128)(2,1)} %param.35) | copy-start | bytes 4515844
  23.4 77.2 %collective-permute-start.1 = (bf16[5,98,384]{2,1,0:T(8,128)(2,1)}, bf16[5,98,384]{2,1,0:T(8,128)(2,1)}, u32[]{:S(2)}, u32[]{:S(2)}) collective-permute-start(bf16[5,98,384]{2,1,0:T(8,128)(2,1)} %reshape.522), channel_id=1, source_target_pairs={{0,2},{2,0},{1,3},{3,1},{4,6},{6,4},{5,7},{7,5},{8,10},{10,8},{9,1... | collective-permute-start | bytes 1128968 | tf_op jit(solution)/shard_map/ppermute | solution.py:635
  82.4 35.9 %collective-permute-start = (bf16[5,196,576]{2,1,0:T(8,128)(2,1)}, bf16[5,196,576]{2,1,0:T(8,128)(2,1)S(1)}, u32[]{:S(2)}, u32[]{:S(2)}) collective-permute-start(bf16[5,196,576]{2,1,0:T(8,128)(2,1)} %reshape.518), channel_id=1, source_target_pairs={{0,2},{2,0},{1,3},{3,1},{4,6},{6,4},{5,7},{7,5},{8,10},{10,8},{9,1... | collective-permute-start | bytes 3386888 | tf_op jit(solution)/shard_map/ppermute | solution.py:635
  170.5 12.8 %collective-permute-start.2 = (bf16[5,196,192]{2,1,0:T(8,128)(2,1)}, bf16[5,196,192]{2,1,0:T(8,128)(2,1)S(1)}, u32[]{:S(2)}, u32[]{:S(2)}) collective-permute-start(bf16[5,196,192]{2,1,0:T(8,128)(2,1)} %get-tuple-element.61), channel_id=1, source_target_pairs={{0,2},{2,0},{1,3},{3,1},{4,6},{6,4},{5,7},{7,5},{8,10},{10,8},{9,1... | collective-permute-start | bytes 1128968 | tf_op jit(solution)/shard_map/ppermute | solution.py:635
  188.3 5.5 %collective-permute-start.3 = (bf16[980,768]{1,0:T(8,128)(2,1)}, bf16[980,768]{1,0:T(8,128)(2,1)}, u32[]{:S(2)}, u32[]{:S(2)}) collective-permute-start(bf16[980,768]{1,0:T(8,128)(2,1)} %convolution_convert_fusion.3), channel_id=1, source_target_pairs={{0,1},{1,0},{2,3},{3,2},{4,5},{5,4},{6,7},{7,6},{8,9},{9,8},{10,11... | collective-permute-start | bytes 4515848 | tf_op jit(solution)/shard_map/ppermute | solution.py:635
  197.4 17.5 %copy-start.8 = (bf16[980,768]{1,0:T(8,128)(2,1)S(1)}, bf16[980,768]{1,0:T(8,128)(2,1)}, u32[]{:S(2)}) copy-start(bf16[980,768]{1,0:T(8,128)(2,1)} %reshape.527) | copy-start | bytes 4515844
  224.6 11.5 %collective-permute-start.5 = (bf16[980,768]{1,0:T(8,128)(2,1)S(1)}, bf16[980,768]{1,0:T(8,128)(2,1)S(1)}, u32[]{:S(2)}, u32[]{:S(2)}) collective-permute-start(bf16[980,768]{1,0:T(8,128)(2,1)S(1)} %fusion.23), channel_id=1, source_target_pairs={{0,1},{1,0},{2,3},{3,2},{4,5},{5,4},{6,7},{7,6},{8,9},{9,8},{10,11... | collective-permute-start | bytes 4515848 | tf_op jit(solution)/shard_map/ppermute | solution.py:635
  227.7 9.7 %collective-permute-start.4 = (bf16[980,768]{1,0:T(8,128)(2,1)S(1)}, bf16[980,768]{1,0:T(8,128)(2,1)S(1)}, u32[]{:S(2)}, u32[]{:S(2)}) collective-permute-start(bf16[980,768]{1,0:T(8,128)(2,1)S(1)} %fusion.26), channel_id=1, source_target_pairs={{0,1},{1,0},{2,3},{3,2},{4,5},{5,4},{6,7},{7,6},{8,9},{9,8},{10,11... | collective-permute-start | bytes 4515848 | tf_op jit(solution)/shard_map/ppermute | solution.py:635
  260.9 16.7 %collective-permute-start.6 = (bf16[5,196,192]{2,1,0:T(8,128)(2,1)}, bf16[5,196,192]{2,1,0:T(8,128)(2,1)}, u32[]{:S(2)}, u32[]{:S(2)}) collective-permute-start(bf16[5,196,192]{2,1,0:T(8,128)(2,1)} %get-tuple-element.161), channel_id=1, source_target_pairs={{0,2},{2,0},{1,3},{3,1},{4,6},{6,4},{5,7},{7,5},{8,10},{10,8},{9,1... | collective-permute-start | bytes 1128968 | tf_op jit(solution)/shard_map/ppermute | solution.py:635
  264.6 88.6 %copy-start.38 = (f32[2]{0:T(128)}, f32[2]{0:T(128)S(1)}, u32[]{:S(2)}) copy-start(f32[2]{0:T(128)S(1)} %compare_convert_fusion) | copy-start | bytes 28
  351.3 10.1 %copy-start.26 = (f32[49,13,1]{0,1,2:T(8,128)S(1)}, f32[49,13,1]{0,1,2:T(8,128)}, u32[]{:S(2)}) copy-start(f32[49,13,1]{0,1,2:T(8,128)} %constant.216) | copy-start | bytes 7648
  351.3 49.0 %collective-permute-start.7 = (bf16[5,196,576]{2,1,0:T(8,128)(2,1)}, bf16[5,196,576]{2,1,0:T(8,128)(2,1)}, u32[]{:S(2)}, u32[]{:S(2)}) collective-permute-start(bf16[5,196,576]{2,1,0:T(8,128)(2,1)} %get-tuple-element.69), channel_id=1, source_target_pairs={{0,2},{2,0},{1,3},{3,1},{4,6},{6,4},{5,7},{7,5},{8,10},{10,8},{9,1... | collective-permute-start | bytes 3386888 | tf_op jit(solution)/shard_map/ppermute | solution.py:635
  361.1 37.9 %collective-permute-start.9 = (bf16[5,49,512]{2,1,0:T(8,128)(2,1)}, bf16[5,49,512]{2,1,0:T(8,128)(2,1)}, u32[]{:S(2)}, u32[]{:S(2)}) collective-permute-start(bf16[5,49,512]{2,1,0:T(8,128)(2,1)} %slice.195), channel_id=1, source_target_pairs={{0,2},{2,0},{1,3},{3,1},{4,6},{6,4},{5,7},{7,5},{8,10},{10,8},{9,1... | collective-permute-start | bytes 752648 | tf_op jit(solution)/shard_map/ppermute | solution.py:635
  423.8 12.9 %collective-permute-start.8 = (bf16[980,768]{1,0:T(8,128)(2,1)}, bf16[980,768]{1,0:T(8,128)(2,1)}, u32[]{:S(2)}, u32[]{:S(2)}) collective-permute-start(bf16[980,768]{1,0:T(8,128)(2,1)} %bitcast_convert_fusion), channel_id=1, source_target_pairs={{0,1},{1,0},{2,3},{3,2},{4,5},{5,4},{6,7},{7,6},{8,9},{9,8},{10,11... | collective-permute-start | bytes 4515848 | tf_op jit(solution)/shard_map/ppermute | solution.py:635
  489.2 15.4 %copy-start.1 = (f32[233,96]{0,1:T(8,128)S(1)}, f32[233,96]{0,1:T(8,128)}, u32[]{:S(2)}) copy-start(f32[233,96]{0,1:T(8,128)} %param.48) | copy-start | bytes 268420
  (35 other events, 137.2 us)
Sparse Core Ops, SparseCore 0:
  10.7 61.5 all-gather.2
  75.1 87.7 all-gather.4
  258.7 149.5 reduce-scatter.1
